TPU v7x, 256 devices: a whole 4x4x8 slice. The times are simulated.
256 devices in a mesh: gx: 16 (over y_hi, x, core), gy: 8 (over z), gz: 2 (over y_lo).
Axes of the slice: x: 4, y: 4 (y_hi: 2, y_lo: 2; y = y_hi * 2 + y_lo), z: 8, core: 2. Of those that a mesh axis runs over, the one named last changes fastest.
Arguments:
- e_forward: float32 [3, 256, 256, 256], P(None, 'gx', 'gy', 'gz'), may hold values from -6 to 6
- h_forward: float32 [3, 256, 256, 256], P(None, 'gx', 'gy', 'gz'), may hold values from -6 to 6
- e_adjoint: float32 [3, 256, 256, 256], P(None, 'gx', 'gy', 'gz'), may hold values from -6 to 6
- h_adjoint: float32 [3, 256, 256, 256], P(None, 'gx', 'gy', 'gz'), may hold values from -6 to 6
- material: int32 [256, 256, 256], P('gx', 'gy', 'gz'), may hold values from 0 to 3
- dft_forward: float32 [3, 2, 3, 96, 256, 256], P(None, None, None, 'gz', 'gx', 'gy'), may hold values from -6 to 6
- dft_adjoint: float32 [3, 2, 3, 96, 256, 256], P(None, None, None, 'gz', 'gx', 'gy'), may hold values from -6 to 6
- angular_freq: float32 [3], replicated, may hold values from 0.05 to 0.6
- layer_map: int32 [96], replicated, may hold values from 0 to 15, as said below
Outputs:
- e_forward_new: float32 [3, 256, 256, 256], P(None, 'gx', 'gy', 'gz')
- h_forward_new: float32 [3, 256, 256, 256], P(None, 'gx', 'gy', 'gz')
- e_adjoint_new: float32 [3, 256, 256, 256], P(None, 'gx', 'gy', 'gz')
- h_adjoint_new: float32 [3, 256, 256, 256], P(None, 'gx', 'gy', 'gz')
- gradient: float32 [16, 256, 256], P('gz', 'gx', 'gy')
Inputs may be any that keep to these rules, and one draw needn't show every extreme that they name: `layer_map`: every design layer owns one contiguous nonempty run of the 96 slab cells; the runs' order along the slab is arbitrary.
All inputs are finite; a program needn't handle non-finite values.
Results may differ from a plain program's by a relative error of at most 0.000073.
Values sent between devices are 32-bit elements; how exact they have to be, the bound alone decides.
A program may use at most 128 MiB of HBM per device.

v0:
```python
import jax
import jax.numpy as jnp
from jax import lax
from jax.sharding import PartitionSpec as P

LAYERS = 16
STEP = 40


PERMITTIVITIES = (1.0, 2.1, 4.0, 12.0)
COURANT = 0.5


def shifted(x, axis, by):
    peers = lax.axis_size(axis)
    return lax.ppermute(x, axis, [(i, (i + by) % peers) for i in range(peers)])


def shifted_2(x, axis, by):
    peers = lax.axis_size(axis)
    pairs = [(i, i + by) for i in range(peers) if 0 <= i + by < peers]
    return lax.ppermute(x, axis, pairs)


def update_coefficient(material):
    result = jnp.zeros(material.shape, jnp.float32)
    for material_id, value_eps in enumerate(PERMITTIVITIES):
        result = result + jnp.where(material == material_id, COURANT / value_eps, 0.0).astype(
            jnp.float32
        )
    return result


def curl_forward(field_e, uppers):
    above_x, above_y, above_z = uppers
    comp_x = (
        above_y[..., 2, :, :, :]
        - field_e[..., 2, :, :, :]
        - (above_z[..., 1, :, :, :] - field_e[..., 1, :, :, :])
    )
    comp_y = (
        above_z[..., 0, :, :, :]
        - field_e[..., 0, :, :, :]
        - (above_x[..., 2, :, :, :] - field_e[..., 2, :, :, :])
    )
    comp_z = (
        above_x[..., 1, :, :, :]
        - field_e[..., 1, :, :, :]
        - (above_y[..., 0, :, :, :] - field_e[..., 0, :, :, :])
    )
    return jnp.stack([comp_x, comp_y, comp_z], axis=-4)


def curl_backward(field_h, lowers):
    below_x, below_y, below_z = lowers
    comp_x = (
        field_h[..., 2, :, :, :]
        - below_y[..., 2, :, :, :]
        - (field_h[..., 1, :, :, :] - below_z[..., 1, :, :, :])
    )
    comp_y = (
        field_h[..., 0, :, :, :]
        - below_z[..., 0, :, :, :]
        - (field_h[..., 2, :, :, :] - below_x[..., 2, :, :, :])
    )
    comp_z = (
        field_h[..., 1, :, :, :]
        - below_x[..., 1, :, :, :]
        - (field_h[..., 0, :, :, :] - below_y[..., 0, :, :, :])
    )
    return jnp.stack([comp_x, comp_y, comp_z], axis=-4)


def shards(
    e_forward,
    h_forward,
    e_adjoint,
    h_adjoint,
    material,
    dft_forward,
    dft_adjoint,
    angular_freq,
    layer_map,
):
    coefficient = update_coefficient(material)
    depth = e_forward.shape[3]
    gz_index = lax.axis_index("gz")
    gz_count = lax.axis_size("gz")
    both_e = jnp.stack([e_forward, e_adjoint])
    both_h = jnp.stack([h_forward, h_adjoint])
    from_x = shifted(both_e[:, :, :1], "gx", -1)
    from_y = shifted(both_e[:, :, :, :1], "gy", -1)
    from_z = shifted_2(both_e[:, :, :, :, :1], "gz", -1)
    uppers = (
        jnp.concatenate([both_e[:, :, 1:], from_x], axis=2),
        jnp.concatenate([both_e[:, :, :, 1:], from_y], axis=3),
        jnp.concatenate([both_e[:, :, :, :, 1:], from_z], axis=4),
    )
    new_h = both_h - COURANT * curl_forward(both_e, uppers)
    into_x = shifted(new_h[:, :, -1:], "gx", 1)
    into_y = shifted(new_h[:, :, :, -1:], "gy", 1)
    into_z = shifted_2(new_h[:, :, :, :, -1:], "gz", 1)
    lowers = (
        jnp.concatenate([into_x, new_h[:, :, :-1]], axis=2),
        jnp.concatenate([into_y, new_h[:, :, :, :-1]], axis=3),
        jnp.concatenate([into_z, new_h[:, :, :, :, :-1]], axis=4),
    )
    new_e = both_e + coefficient * curl_backward(new_h, lowers)
    slab_half = dft_forward.shape[3]
    slab_offset = (1 - gz_index) * (depth - slab_half)
    slab_cells = lax.dynamic_slice_in_dim(new_e, slab_offset, slab_half, axis=4)
    slab_cells = jnp.transpose(slab_cells, (0, 1, 4, 2, 3))
    phases = angular_freq * STEP
    cosine = jnp.cos(phases)[:, None, None, None, None]
    sine_term = jnp.sin(phases)[:, None, None, None, None]
    real_fwd = dft_forward[:, 0] + cosine * slab_cells[0][None]
    imag_fwd = dft_forward[:, 1] - sine_term * slab_cells[0][None]
    real_adj = dft_adjoint[:, 0] + cosine * slab_cells[1][None]
    imag_adj = dft_adjoint[:, 1] - sine_term * slab_cells[1][None]
    products = jnp.sum(real_fwd * real_adj - imag_fwd * imag_adj, axis=(0, 1))
    layer_ids = jnp.arange(LAYERS, dtype=jnp.int32)[:, None]
    local_map = lax.dynamic_slice_in_dim(layer_map, gz_index * slab_half, slab_half)
    local_onehot = (local_map[None, :] == layer_ids).astype(jnp.float32)
    partial_sums = jnp.einsum(
        "ls,sxy->lxy", local_onehot, products, precision=lax.Precision.HIGHEST
    )
    owned_sums = lax.psum_scatter(partial_sums, "gz", scatter_dimension=0, tiled=True)
    thickness = jnp.sum((layer_map[None, :] == layer_ids).astype(jnp.float32), axis=1)
    owned_count = LAYERS // gz_count
    owned_thickness = lax.dynamic_slice_in_dim(thickness, gz_index * owned_count, owned_count)
    gradient = owned_sums / (3.0 * owned_thickness)[:, None, None]
    return (new_e[0], new_h[0], new_e[1], new_h[1], gradient)


def solution(mesh):
    in_specs = (
        P(None, "gx", "gy", "gz"),
        P(None, "gx", "gy", "gz"),
        P(None, "gx", "gy", "gz"),
        P(None, "gx", "gy", "gz"),
        P("gx", "gy", "gz"),
        P(None, None, None, "gz", "gx", "gy"),
        P(None, None, None, "gz", "gx", "gy"),
        P(),
        P(),
    )
    out_specs = (
        P(None, "gx", "gy", "gz"),
        P(None, "gx", "gy", "gz"),
        P(None, "gx", "gy", "gz"),
        P(None, "gx", "gy", "gz"),
        P("gz", "gx", "gy"),
    )
    return jax.shard_map(shards, mesh=mesh, in_specs=in_specs, out_specs=out_specs, check_vma=False)
```

profile of v0, /device:TPU:16, one launch (start us, length us, event | category | flops | bytes accessed | tf_op | source)
XLA Modules:
  0.0 87.1 jit_solution(17705125779681856393)
XLA Ops:
  7.2 1.5 %fusion.6 = f32[2,3,16,32,1]{4,3,2,1,0:T(8,128)S(1)} fusion(f32[1,3,16,32,128]{4,3,2,1,0:T(8,128)} %bitcast.64, f32[1,3,16,32,128]{4,3,2,1,0:T(8,128)} %bitcast.56), kind=kLoop, calls=%fused_computation.29 | loop fusion | flops 3072 | bytes 1585152 | tf_op jit(solution)/shard_map/stack | solution.py:89
  8.7 1.2 %copy.79 = f32[2,3,16,32,1]{3,2,4,1,0:T(8,128)} copy(f32[2,3,16,32,1]{4,3,2,1,0:T(8,128)S(1)} %fusion.6) | data formatting | bytes 24576
  10.0 1.3 %collective-permute-start.1 = (f32[2,3,16,32,1]{3,2,4,1,0:T(8,128)}, f32[2,3,16,32,1]{3,2,4,1,0:T(8,128)}, u32[]{:S(2)}, u32[]{:S(2)}) collective-permute-start(f32[2,3,16,32,1]{3,2,4,1,0:T(8,128)} %copy.79), channel_id=1, source_target_pairs={{1,0},{3,2},{5,4},{7,6},{9,8},{11,10},{13,12},{15,14},{17,16},{19,... | collective-permute-start | bytes 36872 | tf_op jit(solution)/shard_map/ppermute | solution.py:22
  11.9 2.0 %collective-permute-start.2 = (f32[2,3,1,32,128]{4,3,2,1,0:T(8,128)}, f32[2,3,1,32,128]{4,3,2,1,0:T(8,128)S(1)}, u32[]{:S(2)}, u32[]{:S(2)}) collective-permute-start(f32[2,3,1,32,128]{4,3,2,1,0:T(8,128)} %fusion.24), channel_id=1, source_target_pairs={{0,240},{16,0},{32,16},{48,32},{64,48},{80,64},{96,80},{112,96},{1... | collective-permute-start | bytes 294920 | tf_op jit(solution)/shard_map/ppermute | solution.py:16
  13.9 0.7 fusion.25
  14.6 5.9 %collective-permute-start = (f32[2,3,16,1,128]{4,2,3,1,0:T(8,128)}, f32[2,3,16,1,128]{4,2,3,1,0:T(8,128)S(1)}, u32[]{:S(2)}, u32[]{:S(2)}) collective-permute-start(f32[2,3,16,1,128]{4,2,3,1,0:T(8,128)} %bitcast.17), channel_id=1, source_target_pairs={{0,14},{2,0},{4,2},{6,4},{8,6},{10,8},{12,10},{14,12},{1,15},{3,1}... | collective-permute-start | bytes 147464 | tf_op jit(solution)/shard_map/ppermute | solution.py:16
  20.7 1.6 %fusion.5 = f32[2,3,16,32,127]{4,3,2,1,0:T(8,128)} fusion(f32[1,3,16,32,128]{4,3,2,1,0:T(8,128)S(1)} %bitcast.68, f32[1,3,16,32,128]{4,3,2,1,0:T(8,128)S(1)} %bitcast.60), kind=kLoop, calls=%fused_computation.28 | loop fusion | flops 390144 | bytes 3133440 | tf_op jit(solution)/shard_map/stack | solution.py:89
  22.3 1.3 %fusion.8 = f32[2,3,15,32,128]{4,3,2,1,0:T(8,128)} fusion(f32[1,3,16,32,128]{4,3,2,1,0:T(8,128)S(1)} %bitcast.69, f32[1,3,16,32,128]{4,3,2,1,0:T(8,128)S(1)} %bitcast.61), kind=kLoop, calls=%fused_computation.37 | loop fusion | flops 368640 | bytes 3047424 | tf_op jit(solution)/shard_map/stack | solution.py:89
  23.7 1.2 %multiply_cosine_fusion = (f32[3]{0:T(128)}, f32[3]{0:T(128)}) fusion(f32[3]{0:T(128)} %param.16), kind=kLoop, calls=%fused_computation.83 | loop fusion | flops 3 | bytes 36 | tf_op jit(solution)/shard_map/cos | solution.py:114
  24.9 1.3 %convert_reduce_fusion = f32[16]{0:T(128)} fusion(s32[96]{0:T(128)} %param.17), kind=kLoop, calls=%fused_computation.75 | loop fusion | flops 4592 | bytes 448 | tf_op jit(solution)/shard_map/reduce_sum | solution.py:128
  26.2 1.3 %dynamic-slice_multiply_fusion = f32[8]{0:T(128)} fusion(f32[16]{0:T(128)} %convert_reduce_fusion, s32[]{:T(128)S(6)} %select_n.28), kind=kLoop, calls=%fused_computation.81 | loop fusion | flops 8 | bytes 68 | tf_op jit(solution)/shard_map/mul | solution.py:131
  27.5 1.3 %dynamic_slice.9 = s32[48]{0:T(128)} dynamic-slice(s32[96]{0:T(128)} %param.17, s32[]{:T(128)S(6)} %select_n.26), dynamic_slice_sizes={48} | dynamic-slice | bytes 388 | tf_op jit(solution)/shard_map/dynamic_slice | solution.py:122
  28.8 2.6 %copy.64 = f32[2,3,16,32,1]{4,3,2,1,0:T(8,128)} copy(f32[2,3,16,32,1]{3,2,4,1,0:T(8,128)} %collective-permute-done.1) | data formatting | bytes 24576 | tf_op jit(solution)/shard_map/ppermute | solution.py:22
  31.4 2.7 %fusion.23 = (f32[2,1,16,32,128]{4,3,2,1,0:T(8,128)S(1)}, f32[2,1,16,32,128]{4,3,2,1,0:T(8,128)S(1)}, f32[2,1,16,32,128]{4,3,2,1,0:T(8,128)S(1)}) fusion(f32[2,3,16,32,1]{4,3,2,1,0:T(8,128)} %copy.64, f32[2,3,16,32,127]{4,3,2,1,0:T(8,128)} %fusion.5, f32[2,3,16,1,128]{4,3,2,1,0:T(1,128)S(1)} %bitcast.78, f32[2,3,16,31,128]{4,3,2,1,0:T(8,128)S(1)} %fusion.4, ...), kind=kLoop, calls=%fused_computation.69 | loop fusion | flops 2752512 | bytes 7864320 | tf_op jit(solution)/shard_map/sub | solution.py:37
  34.4 2.2 %copy_subtract_fusion = f32[2,3,16,32,128]{4,2,3,1,0:T(8,128)S(1)} fusion(f32[2,3,16,32,128]{4,3,2,1,0:T(8,128)S(1)} %get-tuple-element.39, f32[2,3,16,32,128]{4,3,2,1,0:T(8,128)S(1)} %get-tuple-element.40), kind=kLoop, calls=%fused_computation.34 | loop fusion | flops 786432 | bytes 4718592 | tf_op jit(solution)/shard_map/sub | solution.py:99
  36.7 1.6 %slice.190 = f32[2,3,16,32,1]{4,2,3,1,0:T(8,128)} slice(f32[2,3,16,32,128]{4,2,3,1,0:T(8,128)S(1)} %copy_subtract_fusion), slice={[0:2], [0:3], [0:16], [0:32], [127:128]} | slice | bytes 24576 | tf_op jit(solution)/shard_map/slice | solution.py:102
  38.3 0.7 slice.193
  39.7 2.7 %copy.67 = f32[2,3,16,32,1]{3,2,4,1,0:T(8,128)} copy(f32[2,3,16,32,1]{4,2,3,1,0:T(8,128)} %slice.190) | data formatting | bytes 24576 | tf_op jit(solution)/shard_map/slice | solution.py:102
  42.3 6.1 %collective-permute-start.4 = (f32[2,3,16,32,1]{3,2,4,1,0:T(8,128)}, f32[2,3,16,32,1]{3,2,4,1,0:T(8,128)}, u32[]{:S(2)}, u32[]{:S(2)}) collective-permute-start(f32[2,3,16,32,1]{3,2,4,1,0:T(8,128)} %copy.67), channel_id=1, source_target_pairs={{0,1},{2,3},{4,5},{6,7},{8,9},{10,11},{12,13},{14,15},{16,17},{18,... | collective-permute-start | bytes 36872 | tf_op jit(solution)/shard_map/ppermute | solution.py:22
  48.6 1.3 %slice.188 = f32[2,3,16,31,128]{4,2,3,1,0:T(8,128)} slice(f32[2,3,16,32,128]{4,2,3,1,0:T(8,128)S(1)} %copy_subtract_fusion), slice={[0:2], [0:3], [0:16], [0:31], [0:128]} | slice | bytes 3047424 | tf_op jit(solution)/shard_map/slice | solution.py:105
  49.9 1.1 %copy.75 = f32[3,16,32,128]{3,2,1,0:T(8,128)} copy(f32[3,16,32,128]{3,1,2,0:T(8,128)S(1)} %get-tuple-element.34) | data formatting | bytes 1572864
  51.0 1.1 %copy.76 = f32[3,16,32,128]{3,2,1,0:T(8,128)} copy(f32[3,16,32,128]{3,1,2,0:T(8,128)S(1)} %get-tuple-element.33) | data formatting | bytes 1572864
  52.1 2.6 %copy.68 = f32[2,3,16,32,1]{4,2,3,1,0:T(8,128)} copy(f32[2,3,16,32,1]{3,2,4,1,0:T(8,128)} %collective-permute-done.4) | data formatting | bytes 24576 | tf_op jit(solution)/shard_map/ppermute | solution.py:22
  54.7 1.6 %collective-permute-done.5 = f32[2,3,1,32,128]{4,2,3,1,0:T(1,128)S(1)} collective-permute-done((f32[2,3,1,32,128]{4,2,3,1,0:T(1,128)}, f32[2,3,1,32,128]{4,2,3,1,0:T(1,128)S(1)}, u32[]{:S(2)}, u32[]{:S(2)}) %collective-permute-start.5) | collective-permute-done | bytes 98336 | tf_op jit(solution)/shard_map/ppermute | solution.py:16
  56.3 2.0 %fusion.17 = (f32[2,1,16,32,128]{4,2,3,1,0:T(8,128)S(1)}, f32[2,1,16,32,128]{4,2,3,1,0:T(8,128)S(1)}, f32[2,1,16,32,128]{4,2,3,1,0:T(8,128)S(1)}) fusion(f32[2,3,16,32,127]{4,2,3,1,0:T(8,128)S(1)} %bitcast.54, f32[2,3,16,32,1]{4,2,3,1,0:T(8,128)} %copy.68, f32[2,3,16,31,128]{4,2,3,1,0:T(8,128)} %slice.188, ...), kind=kLoop, calls=%fused_computation.57 | loop fusion | flops 1966080 | bytes 7864320 | tf_op jit(solution)/shard_map/sub | solution.py:57
  59.9 0.8 slice-done
  60.7 1.3 %slice-done.2 = s8[4194304]{0:T(1024)(128)(4,1)S(1)} async-done(((s8[4718592]{0:T(1024)(128)(4,1)}), s8[4194304]{0:T(1024)(128)(4,1)S(1)}, s32[]{:S(2)}) %slice-start.2) | async-done | bytes 4194328
  62.2 1.5 %fusion.2 = f32[48,16,32]{0,2,1:T(8,128)S(1)} fusion(f32[3,2,3,48,16,32]{3,5,4,2,1,0:T(8,128)S(1)} %bitcast.73, f32[3,2,3,48,16,32]{3,5,4,2,1,0:T(8,128)S(1)} %bitcast.75, f32[3]{0:T(128)S(1)} %copy-done.7, f32[3,48,16,32]{1,3,2,0:T(8,128)S(1)} %get-tuple-element.32, f32[3,48,16,32]{1,3,2,0:T(8,128)S(1)} %get-tuple-element.31, f32[3]{0:T(128)S(1)} %copy-done.6), kind=kLoop, calls=%fused_computation.22 | loop fusion | flops 2629632 | bytes 4227096 | tf_op jit(solution)/shard_map/reduce_sum | solution.py:120
  63.7 1.3 %fusion.27 = f32[16,16,32]{2,0,1:T(8,128)} fusion(f32[48,16,32]{0,2,1:T(8,128)S(1)} %fusion.2, s32[48]{0:T(128)S(1)} %copy-done.8), kind=kOutput, calls=%fused_computation.79 | convolution fusion | flops 4719360 | bytes 131264 | tf_op jit(solution)/shard_map/ls,sxy->lxy/dot_general | solution.py:124
  65.0 1.3 %slice_bitcast_fusion.3 = (f32[3,16,32,128]{3,2,1,0:T(8,128)}, f32[3,16,32,128]{3,2,1,0:T(8,128)}) fusion(f32[2,3,16,32,128]{4,3,2,1,0:T(8,128)S(1)} %fusion.7), kind=kLoop, calls=%fused_computation.41 | loop fusion | bytes 3145728 | tf_op jit(solution)/shard_map/squeeze | solution.py:132
  66.3 12.4 %reduce-scatter.2.cloned.1.call-done = f32[8,16,32]{2,0,1:T(8,128)} async-done(((f32[16,16,32]{2,0,1:T(8,128)}), f32[8,16,32]{2,0,1:T(8,128)}) %reduce-scatter.2.cloned.1.call-update) | async-done | bytes 16400 | tf_op jit(solution)/shard_map/reduce_scatter | solution.py:127
  78.7 0.9 %broadcast_divide_fusion = f32[8,16,32]{2,0,1:T(8,128)S(1)} fusion(f32[8,16,32]{2,0,1:T(8,128)} %reduce-scatter.2.cloned.1.call-done, f32[8]{0:T(128)S(1)} %copy-done.5), kind=kLoop, calls=%fused_computation.74 | loop fusion | flops 4096 | bytes 32800 | tf_op jit(solution)/shard_map/div | solution.py:131
  (48 shorter events, 4.6 us)
Async XLA Ops:
  7.2 71.6 %reduce-scatter.2.cloned.1.call-start = ((), (), s32[]{:S(2)}) async-start(), calls=%async_computation.1 | async-start | bytes 196608 | tf_op jit(solution)/shard_map/reduce_scatter | solution.py:127
  8.7 2.6 %copy-start = (f32[3,16,32,128]{3,2,1,0:T(8,128)S(1)}, f32[3,16,32,128]{3,2,1,0:T(8,128)}, u32[]{:S(2)}) copy-start(f32[3,16,32,128]{3,2,1,0:T(8,128)} %param.11) | copy-start | bytes 2359300
  8.7 2.6 %copy-start.1 = (f32[3,16,32,128]{3,2,1,0:T(8,128)S(1)}, f32[3,16,32,128]{3,2,1,0:T(8,128)}, u32[]{:S(2)}) copy-start(f32[3,16,32,128]{3,2,1,0:T(8,128)} %param.9) | copy-start | bytes 2359300
  10.0 18.8 %collective-permute-start.1 = (f32[2,3,16,32,1]{3,2,4,1,0:T(8,128)}, f32[2,3,16,32,1]{3,2,4,1,0:T(8,128)}, u32[]{:S(2)}, u32[]{:S(2)}) collective-permute-start(f32[2,3,16,32,1]{3,2,4,1,0:T(8,128)} %copy.79), channel_id=1, source_target_pairs={{1,0},{3,2},{5,4},{7,6},{9,8},{11,10},{13,12},{15,14},{17,16},{19,... | collective-permute-start | bytes 36872 | tf_op jit(solution)/shard_map/ppermute | solution.py:22
  11.9 19.5 %collective-permute-start.2 = (f32[2,3,1,32,128]{4,3,2,1,0:T(8,128)}, f32[2,3,1,32,128]{4,3,2,1,0:T(8,128)S(1)}, u32[]{:S(2)}, u32[]{:S(2)}) collective-permute-start(f32[2,3,1,32,128]{4,3,2,1,0:T(8,128)} %fusion.24), channel_id=1, source_target_pairs={{0,240},{16,0},{32,16},{48,32},{64,48},{80,64},{96,80},{112,96},{1... | collective-permute-start | bytes 294920 | tf_op jit(solution)/shard_map/ppermute | solution.py:16
  14.6 16.8 %collective-permute-start = (f32[2,3,16,1,128]{4,2,3,1,0:T(8,128)}, f32[2,3,16,1,128]{4,2,3,1,0:T(8,128)S(1)}, u32[]{:S(2)}, u32[]{:S(2)}) collective-permute-start(f32[2,3,16,1,128]{4,2,3,1,0:T(8,128)} %bitcast.17), channel_id=1, source_target_pairs={{0,14},{2,0},{4,2},{6,4},{8,6},{10,8},{12,10},{14,12},{1,15},{3,1}... | collective-permute-start | bytes 147464 | tf_op jit(solution)/shard_map/ppermute | solution.py:16
  22.3 1.3 %copy-start.4 = (s32[16,32,128]{2,1,0:T(8,128)S(1)}, s32[16,32,128]{2,1,0:T(8,128)}, u32[]{:S(2)}) copy-start(s32[16,32,128]{2,1,0:T(8,128)} %param.13) | copy-start | bytes 786436
  31.4 2.7 %copy-start.2 = (f32[3,16,32,128]{3,2,1,0:T(8,128)S(1)}, f32[3,16,32,128]{3,2,1,0:T(8,128)}, u32[]{:S(2)}) copy-start(f32[3,16,32,128]{3,2,1,0:T(8,128)} %param.12) | copy-start | bytes 2359300
  31.4 2.7 %copy-start.3 = (f32[3,16,32,128]{3,2,1,0:T(8,128)S(1)}, f32[3,16,32,128]{3,2,1,0:T(8,128)}, u32[]{:S(2)}) copy-start(f32[3,16,32,128]{3,2,1,0:T(8,128)} %param.10) | copy-start | bytes 2359300
  42.3 9.8 %collective-permute-start.4 = (f32[2,3,16,32,1]{3,2,4,1,0:T(8,128)}, f32[2,3,16,32,1]{3,2,4,1,0:T(8,128)}, u32[]{:S(2)}, u32[]{:S(2)}) collective-permute-start(f32[2,3,16,32,1]{3,2,4,1,0:T(8,128)} %copy.67), channel_id=1, source_target_pairs={{0,1},{2,3},{4,5},{6,7},{8,9},{10,11},{12,13},{14,15},{16,17},{18,... | collective-permute-start | bytes 36872 | tf_op jit(solution)/shard_map/ppermute | solution.py:22
  48.4 7.9 %collective-permute-start.5 = (f32[2,3,1,32,128]{4,2,3,1,0:T(1,128)}, f32[2,3,1,32,128]{4,2,3,1,0:T(1,128)S(1)}, u32[]{:S(2)}, u32[]{:S(2)}) collective-permute-start(f32[2,3,1,32,128]{4,2,3,1,0:T(1,128)} %slice.193), channel_id=1, source_target_pairs={{0,16},{16,32},{32,48},{48,64},{64,80},{80,96},{96,112},{112,128},... | collective-permute-start | bytes 294920 | tf_op jit(solution)/shard_map/ppermute | solution.py:16
  48.4 6.3 %collective-permute-start.3 = (f32[2,3,16,1,128]{4,2,3,1,0:T(8,128)}, f32[2,3,16,1,128]{4,2,3,1,0:T(8,128)S(1)}, u32[]{:S(2)}, u32[]{:S(2)}) collective-permute-start(f32[2,3,16,1,128]{4,2,3,1,0:T(8,128)} %slice.187), channel_id=1, source_target_pairs={{0,2},{2,4},{4,6},{6,8},{8,10},{10,12},{12,14},{14,0},{1,3},{3,5},... | collective-permute-start | bytes 147464 | tf_op jit(solution)/shard_map/ppermute | solution.py:16
  58.5 2.2 %slice-start = ((s8[4718592]{0:T(1024)(128)(4,1)}), s8[4194304]{0:T(1024)(128)(4,1)S(1)}, s32[]{:S(2)}) async-start(s8[4718592]{0:T(1024)(128)(4,1)} %bitcast.72), calls=%async_computation.2 | async-start | bytes 8388608
  58.5 3.5 %slice-start.2 = ((s8[4718592]{0:T(1024)(128)(4,1)}), s8[4194304]{0:T(1024)(128)(4,1)S(1)}, s32[]{:S(2)}) async-start(s8[4718592]{0:T(1024)(128)(4,1)} %bitcast.74), calls=%async_computation.4 | async-start | bytes 8388608
  58.8 3.2 %slice-start.1 = ((s8[4718592]{0:T(1024)(128)(4,1)}), s8[524288]{0:T(1024)(128)(4,1)S(1)}, s32[]{:S(2)}) async-start(s8[4718592]{0:T(1024)(128)(4,1)} %bitcast.72), calls=%async_computation.3 | async-start | bytes 1048576
  58.8 3.4 %slice-start.3 = ((s8[4718592]{0:T(1024)(128)(4,1)}), s8[524288]{0:T(1024)(128)(4,1)S(1)}, s32[]{:S(2)}) async-start(s8[4718592]{0:T(1024)(128)(4,1)} %bitcast.74), calls=%async_computation.5 | async-start | bytes 1048576
  59.7 2.5 %copy-start.6 = (f32[3]{0:T(128)S(1)}, f32[3]{0:T(128)}, u32[]{:S(2)}) copy-start(f32[3]{0:T(128)} %get-tuple-element.37) | copy-start | bytes 40
  59.7 2.5 %copy-start.7 = (f32[3]{0:T(128)S(1)}, f32[3]{0:T(128)}, u32[]{:S(2)}) copy-start(f32[3]{0:T(128)} %get-tuple-element.38) | copy-start | bytes 40
  62.2 1.5 %copy-start.8 = (s32[48]{0:T(128)S(1)}, s32[48]{0:T(128)}, u32[]{:S(2)}) copy-start(s32[48]{0:T(128)} %dynamic_slice.9) | copy-start | bytes 580
  65.0 13.7 %copy-start.5 = (f32[8]{0:T(128)S(1)}, f32[8]{0:T(128)}, u32[]{:S(2)}) copy-start(f32[8]{0:T(128)} %dynamic-slice_multiply_fusion) | copy-start | bytes 100
Sparse Core Ops, SparseCore 0:
  65.1 13.5 reduce-scatter.1
where the time goes:
time: 88.8 us; the launch traced here: 87.1 us
  local copies, waits for them, and re-layouts  22.4 us (25%)
  other arithmetic  19.9 us (22%)
  starting transfers between devices  15.2 us (17%)
  between operations  14.3 us (16%)
  waiting for transfers between devices  14 us (16%)
  matrix products  1.27 us (1%)
    reduce_scatter x1, waiting for transfers between devices, shards(): lax.psum_scatter(partial_sums, 'gz', scatter_dimension=0, tiled=True)  12.4 us
    ppermute x4, starting transfers between devices, shifted(): return lax.ppermute(x, axis, [(i, (i + by) % peers) for i in range(peers)])  7.83 us
    ppermute x2, starting transfers between devices, shifted_2(): return lax.ppermute(x, axis, pairs)  7.35 us
    unnamed x30, local copies, waits for them, and re-layouts  6.51 us
    another operation x6, other arithmetic, shards(): both_e = jnp.stack([e_forward, e_adjoint])  5.97 us
    ppermute x2, local copies, waits for them, and re-layouts, shifted_2(): return lax.ppermute(x, axis, pairs)  5.18 us
    slice x2, local copies, waits for them, and re-layouts, shards(): into_z = shifted_2(new_h[:, :, :, :, -1:], 'gz', 1)  4.29 us
    sub x1, other arithmetic, curl_forward(): above_y[..., 2, :, :, :] - field_e[..., 2, :, :, :]  2.67 us
  transfers between devices with their start and end apart: 7, of which 2 were waited for; matrix products, arithmetic and copies ran while one was open for 23% of the time, Pallas kernels for 0%

commit v1 on v0

v1 whole, which is shorter than its diff:
```python
import jax
import jax.numpy as jnp
from jax import lax
from jax.experimental import pallas as pl
from jax.experimental.pallas import tpu as pltpu
from jax.sharding import PartitionSpec as P

LAYERS = 16
STEP = 40
COURANT = 0.5
PERMITTIVITIES = (1.0, 2.1, 4.0, 12.0)
MESH = pl.DeviceIdType.MESH
F32 = jnp.float32
QUARTERS = 4


def step_kernel(
    ef, hf, ea, ha, mat, df, da, freq, lmap,
    ebuf, hbuf, grad,
    matb, dfb, dab, freqb, lmapb, ubuf, vbuf, gbuf, prod,
    ysend, zsend, xh, yh, zh, ysend2, zsend2, xh2, yh2, zh2, part_out, part_in,
    lsem, dsem, ssem, rsem,
):
    nx, ny, nz = mat.shape
    slab = df.shape[5]
    owned = LAYERS // 2
    gx, gy, gz = lax.axis_index("gx"), lax.axis_index("gy"), lax.axis_index("gz")
    sx, sy = lax.axis_size("gx"), lax.axis_size("gy")
    x_up, x_down = lax.rem(gx + 1, sx), lax.rem(gx + sx - 1, sx)
    y_up, y_down = lax.rem(gy + 1, sy), lax.rem(gy + sy - 1, sy)
    z_other = 1 - gz

    loads = [
        pltpu.make_async_copy(ef, ebuf.at[0, :, 0:nx, 0:ny, :], lsem.at[0]),
        pltpu.make_async_copy(ea, ebuf.at[1, :, 0:nx, 0:ny, :], lsem.at[1]),
        pltpu.make_async_copy(hf, hbuf.at[0, :, 1 : nx + 1, 8 : ny + 8, :], lsem.at[2]),
        pltpu.make_async_copy(ha, hbuf.at[1, :, 1 : nx + 1, 8 : ny + 8, :], lsem.at[3]),
        pltpu.make_async_copy(freq, freqb, lsem.at[4]),
        pltpu.make_async_copy(lmap, lmapb, lsem.at[5]),
        pltpu.make_async_copy(mat, matb, lsem.at[6]),
    ]
    for load in loads:
        load.start()
    rows = nx // QUARTERS
    dft_loads = []
    for q in range(QUARTERS):
        part = pl.ds(q * rows, rows)
        pair = (
            pltpu.make_async_copy(df.at[:, :, :, part], dfb.at[:, :, :, part], dsem.at[0, q]),
            pltpu.make_async_copy(da.at[:, :, :, part], dab.at[:, :, :, part], dsem.at[1, q]),
        )
        for load in pair:
            load.start()
        dft_loads.append(pair)

    barrier = pltpu.get_barrier_semaphore()
    for peer in ({"gx": x_up}, {"gx": x_down}, {"gy": y_up}, {"gy": y_down}, {"gz": z_other}):
        pl.semaphore_signal(barrier, inc=1, device_id=peer, device_id_type=MESH)

    lane = lax.broadcasted_iota(jnp.int32, (ny, nz), 1)

    def send(index, src, dst, peer):
        copy = pltpu.make_async_remote_copy(
            src_ref=src, dst_ref=dst, send_sem=ssem.at[index], recv_sem=rsem.at[index],
            device_id=peer, device_id_type=MESH,
        )
        copy.start()
        return copy

    def gather_lane(buf, x_off, y_off, from_lane):
        def body(x, acc):
            for r in range(2):
                for c in range(2):
                    k = (r * 2 + c) * nx + x
                    tile = buf[r, c, x + x_off, y_off : y_off + ny, :]
                    moved = pltpu.roll(tile, lax.rem(k - from_lane + nz, nz), 1)
                    acc = jnp.where(lane == k, moved, acc)
            return acc

        return lax.fori_loop(0, nx, body, jnp.zeros((ny, nz), F32))

    loads[0].wait()
    loads[1].wait()
    for r in range(2):
        for i, c in enumerate((0, 2)):
            ysend[r, i] = ebuf[r, c, 0:nx, 0, :]
    zsend[...] = gather_lane(ebuf, 0, 0, 0)
    pl.semaphore_wait(barrier, 5)
    first = [
        send(0, ebuf.at[:, 1:3, 0, 0:ny, :], xh, {"gx": x_down}),
        send(1, ysend, yh, {"gy": y_down}),
        send(2, zsend, zh, {"gz": z_other}),
    ]

    loads[4].wait()
    loads[5].wait()
    cosine, sine = [], []
    squares = None
    for f in range(df.shape[0]):
        phase = jnp.full((8, slab), freqb[f] * STEP, F32)
        cos_f, sin_f = jnp.cos(phase)[0:1], jnp.sin(phase)[0:1]
        cosine.append(cos_f)
        sine.append(sin_f)
        term = cos_f * cos_f - sin_f * sin_f
        squares = term if squares is None else squares + term
    layer_map = lmapb[...].reshape(1, 2 * slab)
    layer_ids = lax.broadcasted_iota(jnp.int32, (LAYERS, 2 * slab), 0)
    onehot_all = (layer_map == layer_ids).astype(F32)
    thickness = jnp.sum(onehot_all, axis=1, keepdims=True)
    low = gz == 0
    own_thickness = 3.0 * jnp.where(low, thickness[0:owned], thickness[owned:LAYERS])
    onehot = jnp.where(low, onehot_all[:, 0:slab], onehot_all[:, slab : 2 * slab])

    loads[2].wait()
    loads[3].wait()
    for copy in first:
        copy.wait()
    for r in range(2):
        for i in range(2):
            ebuf[r, 1 + i, nx, 0:ny, :] = xh[r, i]
            ebuf[r, 2 * i, 0:nx, ny, :] = yh[r, i]

    z_above = jnp.where(low, zh[...], 0.0)

    def h_plane(x, carry):
        for r in range(2):
            e0 = ebuf[r, 0, x, 0:ny, :]
            e1 = ebuf[r, 1, x, 0:ny, :]
            e2 = ebuf[r, 2, x, 0:ny, :]

            def up_z(value, c):
                k = (r * 2 + c) * nx + x
                edge = pltpu.roll(z_above, nz - 1 - k, 1)
                return jnp.where(lane == nz - 1, edge, pltpu.roll(value, nz - 1, 1))

            curl_x = (ebuf[r, 2, x, 1 : ny + 1, :] - e2) - (up_z(e1, 1) - e1)
            curl_y = (up_z(e0, 0) - e0) - (ebuf[r, 2, x + 1, 0:ny, :] - e2)
            curl_z = (ebuf[r, 1, x + 1, 0:ny, :] - e1) - (ebuf[r, 0, x, 1 : ny + 1, :] - e0)
            for c, curl in enumerate((curl_x, curl_y, curl_z)):
                hbuf[r, c, x + 1, 8 : ny + 8, :] = hbuf[r, c, x + 1, 8 : ny + 8, :] - COURANT * curl
        return carry

    lax.fori_loop(0, nx, h_plane, 0)

    for r in range(2):
        for i, c in enumerate((0, 2)):
            ysend2[r, i] = hbuf[r, c, 1 : nx + 1, ny + 7, :]
    zsend2[...] = gather_lane(hbuf, 1, 8, nz - 1)
    second = [
        send(3, hbuf.at[:, 1:3, nx, 8 : ny + 8, :], xh2, {"gx": x_up}),
        send(4, ysend2, yh2, {"gy": y_up}),
        send(5, zsend2, zh2, {"gz": z_other}),
    ]

    def dft_plane(x, carry):
        total = None
        for c in range(3):
            u = v = None
            for f in range(df.shape[0]):
                rf, mf = dfb[f, 0, c, x], dfb[f, 1, c, x]
                ra, ma = dab[f, 0, c, x], dab[f, 1, c, x]
                base = rf * ra - mf * ma
                total = base if total is None else total + base
                u_f = cosine[f] * ra + sine[f] * ma
                v_f = cosine[f] * rf + sine[f] * mf
                u = u_f if u is None else u + u_f
                v = v_f if v is None else v + v_f
            ubuf[c, x] = u
            vbuf[c, x] = v
        gbuf[x] = total
        return carry

    for q in range(QUARTERS):
        for load in dft_loads[q]:
            load.wait()
        lax.fori_loop(q * rows, (q + 1) * rows, dft_plane, 0)

    loads[6].wait()
    for copy in second:
        copy.wait()
    for r in range(2):
        for i in range(2):
            hbuf[r, 1 + i, 0, 8 : ny + 8, :] = xh2[r, i]
            hbuf[r, 2 * i, 1 : nx + 1, 7, :] = yh2[r, i]

    z_below = jnp.where(low, 0.0, zh2[...])
    shift = slab * z_other

    def e_plane(x, carry):
        m = matb[x]
        coefficient = jnp.where(
            m == 0, COURANT / PERMITTIVITIES[0],
            jnp.where(m == 1, COURANT / PERMITTIVITIES[1],
                      jnp.where(m == 2, COURANT / PERMITTIVITIES[2], COURANT / PERMITTIVITIES[3])),
        ).astype(F32)
        cells = []
        for r in range(2):
            h0 = hbuf[r, 0, x + 1, 8 : ny + 8, :]
            h1 = hbuf[r, 1, x + 1, 8 : ny + 8, :]
            h2 = hbuf[r, 2, x + 1, 8 : ny + 8, :]

            def down_z(value, c):
                k = (r * 2 + c) * nx + x
                edge = pltpu.roll(z_below, lax.rem(nz - k, nz), 1)
                return jnp.where(lane == 0, edge, pltpu.roll(value, 1, 1))

            curl_x = (h2 - hbuf[r, 2, x + 1, 7 : ny + 7, :]) - (h1 - down_z(h1, 1))
            curl_y = (h0 - down_z(h0, 0)) - (h2 - hbuf[r, 2, x, 8 : ny + 8, :])
            curl_z = (h1 - hbuf[r, 1, x, 8 : ny + 8, :]) - (h0 - hbuf[r, 0, x + 1, 7 : ny + 7, :])
            fields = []
            for c, curl in enumerate((curl_x, curl_y, curl_z)):
                new_e = ebuf[r, c, x, 0:ny, :] + coefficient * curl
                ebuf[r, c, x, 0:ny, :] = new_e
                fields.append(pltpu.roll(new_e, shift, 1)[:, 0:slab])
            cells.append(fields)
        total = gbuf[x]
        for c in range(3):
            fwd, adj = cells[0][c], cells[1][c]
            total = total + (fwd * (ubuf[c, x] + squares * adj) + adj * vbuf[c, x])
        prod[pl.ds(pl.multiple_of(x * ny, ny), ny), :] = total
        return carry

    lax.fori_loop(0, nx, e_plane, 0)

    sums = lax.dot_general(
        onehot, prod[...], (((1,), (1,)), ((), ())),
        precision=lax.Precision.HIGHEST, preferred_element_type=F32,
    )
    part_out[...] = jnp.where(low, sums[owned:LAYERS], sums[0:owned])
    last = send(6, part_out, part_in, {"gz": z_other})
    mine = jnp.where(low, sums[0:owned], sums[owned:LAYERS])
    last.wait()
    result = (mine + part_in[...]) / own_thickness
    for x in range(nx):
        grad[:, x, :] = result[:, x * ny : (x + 1) * ny]


def store_kernel(ebuf, hbuf, grad, oef, ohf, oea, oha, ograd, sem):
    nx, ny = oef.shape[1:3]
    copies = [
        pltpu.make_async_copy(ebuf.at[0, :, 0:nx, 0:ny, :], oef, sem.at[0]),
        pltpu.make_async_copy(hbuf.at[0, :, 1 : nx + 1, 8 : ny + 8, :], ohf, sem.at[1]),
        pltpu.make_async_copy(ebuf.at[1, :, 0:nx, 0:ny, :], oea, sem.at[2]),
        pltpu.make_async_copy(hbuf.at[1, :, 1 : nx + 1, 8 : ny + 8, :], oha, sem.at[3]),
        pltpu.make_async_copy(grad, ograd, sem.at[4]),
    ]
    for copy in copies:
        copy.start()
    for copy in copies:
        copy.wait()


def shards(ef, hf, ea, ha, mat, df, da, freq, lmap):
    comps, nx, ny, nz = ef.shape
    freqs, _, _, slab = df.shape[:4]
    df = jnp.transpose(df, (0, 1, 2, 4, 5, 3))
    da = jnp.transpose(da, (0, 1, 2, 4, 5, 3))
    args = [pltpu.with_memory_space_constraint(a, pltpu.HBM) for a in (ef, hf, ea, ha, mat, df, da, freq, lmap)]
    hbm = pl.BlockSpec(memory_space=pltpu.HBM)
    vmem = pl.BlockSpec(memory_space=pltpu.VMEM)
    padded = (2, comps, nx + 1, ny + 8, nz)
    owned = LAYERS // 2
    out = pl.pallas_call(
        step_kernel,
        name="yee_step",
        out_shape=(
            pltpu.VMEM(padded, F32),
            pltpu.VMEM(padded, F32),
            pltpu.VMEM((owned, nx, ny), F32),
        ),
        in_specs=[hbm] * 9,
        out_specs=[vmem] * 3,
        scratch_shapes=[
            pltpu.VMEM((nx, ny, nz), jnp.int32),
            pltpu.VMEM(df.shape, F32),
            pltpu.VMEM(da.shape, F32),
            pltpu.SMEM(freq.shape, F32),
            pltpu.VMEM(lmap.shape, jnp.int32),
            pltpu.VMEM((comps, nx, ny, slab), F32),
            pltpu.VMEM((comps, nx, ny, slab), F32),
            pltpu.VMEM((nx, ny, slab), F32),
            pltpu.VMEM((nx * ny, slab), F32),
            pltpu.VMEM((2, 2, nx, nz), F32),
            pltpu.VMEM((ny, nz), F32),
            pltpu.VMEM((2, 2, ny, nz), F32),
            pltpu.VMEM((2, 2, nx, nz), F32),
            pltpu.VMEM((ny, nz), F32),
            pltpu.VMEM((2, 2, nx, nz), F32),
            pltpu.VMEM((ny, nz), F32),
            pltpu.VMEM((2, 2, ny, nz), F32),
            pltpu.VMEM((2, 2, nx, nz), F32),
            pltpu.VMEM((ny, nz), F32),
            pltpu.VMEM((owned, nx * ny), F32),
            pltpu.VMEM((owned, nx * ny), F32),
            pltpu.SemaphoreType.DMA((7,)),
            pltpu.SemaphoreType.DMA((2, QUARTERS)),
            pltpu.SemaphoreType.DMA((7,)),
            pltpu.SemaphoreType.DMA((7,)),
        ],
        compiler_params=pltpu.CompilerParams(
            collective_id=0, has_side_effects=True, vmem_limit_bytes=24 << 20
        ),
    )(*args)
    staged = [pltpu.with_memory_space_constraint(o, pltpu.VMEM) for o in out]
    field = jax.ShapeDtypeStruct(ef.shape, F32)
    return pl.pallas_call(
        store_kernel,
        name="store_fields",
        out_shape=(field, field, field, field, jax.ShapeDtypeStruct((owned, nx, ny), F32)),
        in_specs=[vmem] * 3,
        out_specs=[hbm] * 5,
        scratch_shapes=[pltpu.SemaphoreType.DMA((5,))],
        compiler_params=pltpu.CompilerParams(vmem_limit_bytes=1 << 20),
    )(*staged)


def solution(mesh):
    field = P(None, "gx", "gy", "gz")
    dft = P(None, None, None, "gz", "gx", "gy")
    in_specs = (field, field, field, field, P("gx", "gy", "gz"), dft, dft, P(), P())
    out_specs = (field, field, field, field, P("gz", "gx", "gy"))
    return jax.shard_map(shards, mesh=mesh, in_specs=in_specs, out_specs=out_specs, check_vma=False)
```

time: 88.8 us -> 27.6 us (0.31); the launches traced: 87.1 us -> 27.5 us
  Pallas kernels: 0 us -> 26.9 us
  local copies, waits for them, and re-layouts: 22.4 us -> 0 us
  other arithmetic: 19.9 us -> 0 us
  starting transfers between devices: 15.2 us -> 0 us
  waiting for transfers between devices: 14 us -> 0 us
  between operations: 14.3 us -> 0.64 us
  matrix products: 1.27 us -> 0 us
    pallas_call x0 -> x2, Pallas kernels: none -> 26.9 us  [the longest x1 25.2 us: shards(): pl.pallas_call(step_kernel, name='yee_step', out_shape=(pltpu.VMEM(padded...]
    ppermute x6 -> x0, starting transfers between devices: 15.2 us -> none  [the longest x4 7.83 us: shifted(): return lax.ppermute(x, axis, [(i, (i + by) % peers) for i in range(peers)])]
    reduce_scatter x1 -> x0, waiting for transfers between devices: 12.4 us -> none  [shards(): lax.psum_scatter(partial_sums, 'gz', scatter_dimension=0, tiled=True)]
    sub x3 -> x0, other arithmetic: 6.94 us -> none  [the longest x1 2.67 us: curl_forward(): above_y[..., 2, :, :, :] - field_e[..., 2, :, :, :]]
    slice x5 -> x0, local copies, waits for them, and re-layouts: 6.9 us -> none  [the longest x2 4.29 us: shards(): into_z = shifted_2(new_h[:, :, :, :, -1:], 'gz', 1)]
    unnamed x30 -> x0, local copies, waits for them, and re-layouts: 6.51 us -> none
    another operation x7 -> x0, other arithmetic: 6.28 us -> none  [the longest x6 5.97 us: shards(): both_e = jnp.stack([e_forward, e_adjoint])]
    ppermute x2 -> x0, local copies, waits for them, and re-layouts: 5.18 us -> none  [shifted_2(): return lax.ppermute(x, axis, pairs)]
  transfers between devices with their start and end apart: 7 -> 0, of which waited for: 2 -> 0; matrix products, arithmetic and copies ran while one was open for 23% -> 0% of each run, Pallas kernels for 0% -> 0%
where the time goes in v1:
time: 27.6 us; the launch traced here: 27.5 us
  Pallas kernels  26.9 us (97%)
  between operations  0.64 us (2%)
    pallas_call x1, Pallas kernels, shards(): pl.pallas_call(step_kernel, name='yee_step', out_shape=(pltpu.VMEM(padded...  25.2 us
    pallas_call x1, Pallas kernels, shards(): pl.pallas_call(store_kernel, name='store_fields', out_shape=(field, field...  1.71 us

profile of v1, /device:TPU:16, one launch (start us, length us, event | category | flops | bytes accessed | tf_op | source)
XLA Modules:
  0.0 27.5 jit_solution(2837747583602997003)
XLA Ops:
  0.6 25.2 %yee_step.1 = (f32[2,3,17,40,128]{4,3,2,1,0:T(8,128)S(1)}, f32[2,3,17,40,128]{4,3,2,1,0:T(8,128)S(1)}, f32[8,16,32]{2,1,0:T(8,128)S(1)}) custom-call(f32[3,16,32,128]{3,2,1,0:T(8,128)} %ef.1, f32[3,16,32,128]{3,2,1,0:T(8,128)} %hf.1, f32[3,16,32,128]{3,2,1,0:T(8,128)} %ea.1, f32[3,16,32,128]{3,2,1,0:T(8,128)} %ha.1, s32[16,32,128]{2,1,0:T(8,128)} %mat.1, ...), custom_call_target="tpu_custom_call" | custom-call | tf_op jit(solution)/shard_map/yee_step/pallas_call | solution.py:263
  25.8 1.7 %store_fields.1 = (f32[3,16,32,128]{3,2,1,0:T(8,128)}, f32[3,16,32,128]{3,2,1,0:T(8,128)}, f32[3,16,32,128]{3,2,1,0:T(8,128)}, f32[3,16,32,128]{3,2,1,0:T(8,128)}, f32[8,16,32]{2,1,0:T(8,128)}) custom-call(f32[2,3,17,40,128]{4,3,2,1,0:T(8,128)S(1)} %get-tuple-element.8.ebuf, f32[2,3,17,40,128]{4,3,2,1,0:T(8,128)S(1)} %get-tuple-element.9.hbuf, ...), custom_call_target="tpu_custom_call" | custom-call | tf_op jit(solution)/shard_map/store_fields/pallas_call | solution.py:306

commit v2 on v1

--- a/solution.py
+++ b/solution.py
@@ -18,17 +18,21 @@
     ef, hf, ea, ha, mat, df, da, freq, lmap,
     ebuf, hbuf, grad,
     matb, dfb, dab, freqb, lmapb, ubuf, vbuf, gbuf, prod,
-    ysend, zsend, xh, yh, zh, ysend2, zsend2, xh2, yh2, zh2, part_out, part_in,
+    ye_out, xya_out, xyb_out, xz_out, yz_out, yp_out, z_out, part_out,
+    xe, ye, xya, xyb, xz, yz, xp, yp, zf, part_in,
     lsem, dsem, ssem, rsem,
 ):
     nx, ny, nz = mat.shape
-    slab = df.shape[5]
+    freqs, slab = df.shape[0], df.shape[5]
     owned = LAYERS // 2
     gx, gy, gz = lax.axis_index("gx"), lax.axis_index("gy"), lax.axis_index("gz")
     sx, sy = lax.axis_size("gx"), lax.axis_size("gy")
     x_up, x_down = lax.rem(gx + 1, sx), lax.rem(gx + sx - 1, sx)
     y_up, y_down = lax.rem(gy + 1, sy), lax.rem(gy + sy - 1, sy)
     z_other = 1 - gz
+    low = gz == 0
+    x_cross = lax.rem(gx + sx + 2 * gz - 1, sx)
+    y_cross = lax.rem(gy + sy + 2 * gz - 1, sy)
 
     loads = [
         pltpu.make_async_copy(ef, ebuf.at[0, :, 0:nx, 0:ny, :], lsem.at[0]),
@@ -53,11 +57,20 @@
             load.start()
         dft_loads.append(pair)
 
+    to_xe, to_xp = {"gx": x_down}, {"gx": x_up}
+    to_ye, to_yp = {"gy": y_down}, {"gy": y_up}
+    to_z = {"gz": z_other}
+    to_xya, to_xyb = {"gx": x_up, "gy": y_down}, {"gx": x_down, "gy": y_up}
+    to_xz, to_yz = {"gx": x_cross, "gz": z_other}, {"gy": y_cross, "gz": z_other}
+    peers = (to_xe, to_xp, to_ye, to_yp, to_z, to_xya, to_xyb, to_xz, to_yz)
     barrier = pltpu.get_barrier_semaphore()
-    for peer in ({"gx": x_up}, {"gx": x_down}, {"gy": y_up}, {"gy": y_down}, {"gz": z_other}):
+    for peer in peers:
         pl.semaphore_signal(barrier, inc=1, device_id=peer, device_id_type=MESH)
 
     lane = lax.broadcasted_iota(jnp.int32, (ny, nz), 1)
+    row = lax.broadcasted_iota(jnp.int32, (ny, nz), 0)
+    lane_x = lax.broadcasted_iota(jnp.int32, (nx, nz), 1)
+    row_x = lax.broadcasted_iota(jnp.int32, (nx, nz), 0)
 
     def send(index, src, dst, peer):
         copy = pltpu.make_async_remote_copy(
@@ -67,13 +80,12 @@
         copy.start()
         return copy
 
-    def gather_lane(buf, x_off, y_off, from_lane):
+    def gather_lane(tile_of, from_lane):
         def body(x, acc):
             for r in range(2):
                 for c in range(2):
                     k = (r * 2 + c) * nx + x
-                    tile = buf[r, c, x + x_off, y_off : y_off + ny, :]
-                    moved = pltpu.roll(tile, lax.rem(k - from_lane + nz, nz), 1)
+                    moved = pltpu.roll(tile_of(r, c, x), lax.rem(k - from_lane + nz, nz), 1)
                     acc = jnp.where(lane == k, moved, acc)
             return acc
 
@@ -81,82 +93,109 @@
 
     loads[0].wait()
     loads[1].wait()
+    xz_tile = jnp.zeros((ny, nz), F32)
+    yz_tile = jnp.zeros((nx, nz), F32)
+    yz_row = jnp.zeros((1, nz), F32)
     for r in range(2):
         for i, c in enumerate((0, 2)):
-            ysend[r, i] = ebuf[r, c, 0:nx, 0, :]
-    zsend[...] = gather_lane(ebuf, 0, 0, 0)
-    pl.semaphore_wait(barrier, 5)
-    first = [
-        send(0, ebuf.at[:, 1:3, 0, 0:ny, :], xh, {"gx": x_down}),
-        send(1, ysend, yh, {"gy": y_down}),
-        send(2, zsend, zh, {"gz": z_other}),
-    ]
+            ye_out[r, i] = ebuf[r, c, 0:nx, 0, :]
+        xya_out[r : r + 1, :] = ebuf[r, 0, nx - 1, 0:1, :]
+        xyb_out[r : r + 1, :] = ebuf[r, 1, 0, ny - 1 : ny, :]
+        k = r * 2 * nx + 2 * nx - 1
+        column = jnp.where(
+            low, pltpu.roll(ebuf[r, 2, 0, 0:ny, :], k + 1, 1), pltpu.roll(ebuf[r, 0, nx - 1, 0:ny, :], k, 1)
+        )
+        xz_tile = jnp.where(lane == k, column, xz_tile)
+        column = ebuf[r, 1, 0:nx, ny - 1, :]
+        yz_tile = jnp.where(lane_x == r, column if r == 0 else pltpu.roll(column, r, 1), yz_tile)
+        column = jnp.broadcast_to(ye_out[r, 1][:, nz - 1 : nz], (nx, nz))
+        picked = jnp.where(lane_x == r * 2 * nx + row_x, column, 0.0)
+        yz_row = yz_row + jnp.sum(picked, axis=0, keepdims=True)
+    xz_out[...] = xz_tile
+    yz_out[0:nx, :] = yz_tile
+    yz_out[nx : nx + 8, :] = jnp.broadcast_to(yz_row, (8, nz))
+    pl.semaphore_wait(barrier, len(peers))
+    sent_xya = send(0, xya_out, xya, to_xya)
+    sent_xyb = send(1, xyb_out, xyb, to_xyb)
+    sent_ye = send(2, ye_out, ye, to_ye)
+    sent_xe = send(3, ebuf.at[:, 1:3, 0, 0:ny, :], xe, to_xe)
+    sent_xz = send(4, xz_out, xz, to_xz)
+    sent_yz = send(5, yz_out, yz, to_yz)
+
+    zero_row = jnp.zeros((nx, nz), F32)
+    for r in range(2):
+        ebuf[r, 0, 0:nx, ny, :] = zero_row
+        ebuf[r, 2, 0:nx, ny, :] = zero_row
+    loads[2].wait()
+    loads[3].wait()
+
+    def h_plane(x, last=False):
+        for r in range(2):
+            e0 = ebuf[r, 0, x, 0:ny, :]
+            e1 = ebuf[r, 1, x, 0:ny, :]
+            e2 = ebuf[r, 2, x, 0:ny, :]
+
+            def up_z(value):
+                return jnp.where(lane == nz - 1, 0.0, pltpu.roll(value, nz - 1, 1))
+
+            curl_x = (ebuf[r, 2, x, 1 : ny + 1, :] - e2) - (up_z(e1) - e1)
+            curl_y = up_z(e0) - e0
+            curl_z = ebuf[r, 0, x, 1 : ny + 1, :] - e0
+            if last:
+                curl_y = curl_y + e2
+                curl_z = -e1 - curl_z
+            else:
+                curl_y = curl_y - (ebuf[r, 2, x + 1, 0:ny, :] - e2)
+                curl_z = (ebuf[r, 1, x + 1, 0:ny, :] - e1) - curl_z
+            for c, curl in enumerate((curl_x, curl_y, curl_z)):
+                hbuf[r, c, x + 1, 8 : ny + 8, :] = hbuf[r, c, x + 1, 8 : ny + 8, :] - COURANT * curl
+
+    h_plane(nx - 1, last=True)
+    sent_xp = send(6, hbuf.at[:, 1:3, nx, 8 : ny + 8, :], xp, to_xp)
+
+    def h_body(x, carry):
+        h_plane(x)
+        return carry
+
+    lax.fori_loop(0, nx - 1, h_body, 0)
+    for r in range(2):
+        for i, c in enumerate((0, 2)):
+            yp_out[r, i] = hbuf[r, c, 1 : nx + 1, ny + 7, :]
+    sent_yp = send(7, yp_out, yp, to_yp)
+    first_e = gather_lane(lambda r, c, x: ebuf[r, 1 - c, x, 0:ny, :], 0)
+    last_h = gather_lane(lambda r, c, x: hbuf[r, c, x + 1, 8 : ny + 8, :], nz - 1)
+    z_out[...] = jnp.where(low, last_h, first_e)
+    sent_z = send(8, z_out, zf, to_z)
 
     loads[4].wait()
     loads[5].wait()
     cosine, sine = [], []
     squares = None
-    for f in range(df.shape[0]):
-        phase = jnp.full((8, slab), freqb[f] * STEP, F32)
+    for f in range(freqs):
+        phase = jnp.full((8, nz), freqb[f] * STEP, F32)
         cos_f, sin_f = jnp.cos(phase)[0:1], jnp.sin(phase)[0:1]
-        cosine.append(cos_f)
-        sine.append(sin_f)
+        cosine.append(cos_f[:, 0:slab])
+        sine.append(sin_f[:, 0:slab])
         term = cos_f * cos_f - sin_f * sin_f
         squares = term if squares is None else squares + term
+    shift = (nz - slab) * z_other
     layer_map = lmapb[...].reshape(1, 2 * slab)
     layer_ids = lax.broadcasted_iota(jnp.int32, (LAYERS, 2 * slab), 0)
     onehot_all = (layer_map == layer_ids).astype(F32)
     thickness = jnp.sum(onehot_all, axis=1, keepdims=True)
-    low = gz == 0
     own_thickness = 3.0 * jnp.where(low, thickness[0:owned], thickness[owned:LAYERS])
-    onehot = jnp.where(low, onehot_all[:, 0:slab], onehot_all[:, slab : 2 * slab])
-
-    loads[2].wait()
-    loads[3].wait()
-    for copy in first:
-        copy.wait()
-    for r in range(2):
-        for i in range(2):
-            ebuf[r, 1 + i, nx, 0:ny, :] = xh[r, i]
-            ebuf[r, 2 * i, 0:nx, ny, :] = yh[r, i]
-
-    z_above = jnp.where(low, zh[...], 0.0)
-
-    def h_plane(x, carry):
-        for r in range(2):
-            e0 = ebuf[r, 0, x, 0:ny, :]
-            e1 = ebuf[r, 1, x, 0:ny, :]
-            e2 = ebuf[r, 2, x, 0:ny, :]
-
-            def up_z(value, c):
-                k = (r * 2 + c) * nx + x
-                edge = pltpu.roll(z_above, nz - 1 - k, 1)
-                return jnp.where(lane == nz - 1, edge, pltpu.roll(value, nz - 1, 1))
-
-            curl_x = (ebuf[r, 2, x, 1 : ny + 1, :] - e2) - (up_z(e1, 1) - e1)
-            curl_y = (up_z(e0, 0) - e0) - (ebuf[r, 2, x + 1, 0:ny, :] - e2)
-            curl_z = (ebuf[r, 1, x + 1, 0:ny, :] - e1) - (ebuf[r, 0, x, 1 : ny + 1, :] - e0)
-            for c, curl in enumerate((curl_x, curl_y, curl_z)):
-                hbuf[r, c, x + 1, 8 : ny + 8, :] = hbuf[r, c, x + 1, 8 : ny + 8, :] - COURANT * curl
-        return carry
-
-    lax.fori_loop(0, nx, h_plane, 0)
-
-    for r in range(2):
-        for i, c in enumerate((0, 2)):
-            ysend2[r, i] = hbuf[r, c, 1 : nx + 1, ny + 7, :]
-    zsend2[...] = gather_lane(hbuf, 1, 8, nz - 1)
-    second = [
-        send(3, hbuf.at[:, 1:3, nx, 8 : ny + 8, :], xh2, {"gx": x_up}),
-        send(4, ysend2, yh2, {"gy": y_up}),
-        send(5, zsend2, zh2, {"gz": z_other}),
-    ]
+
+    def place(value):
+        rest = jnp.zeros((value.shape[0], nz - slab), F32)
+        return pltpu.roll(jnp.concatenate([value, rest], axis=1), shift, 1)
+
+    onehot = place(jnp.where(low, onehot_all[:, 0:slab], onehot_all[:, slab : 2 * slab]))
 
     def dft_plane(x, carry):
         total = None
         for c in range(3):
             u = v = None
-            for f in range(df.shape[0]):
+            for f in range(freqs):
                 rf, mf = dfb[f, 0, c, x], dfb[f, 1, c, x]
                 ra, ma = dab[f, 0, c, x], dab[f, 1, c, x]
                 base = rf * ra - mf * ma
@@ -165,26 +204,67 @@
                 v_f = cosine[f] * rf + sine[f] * mf
                 u = u_f if u is None else u + u_f
                 v = v_f if v is None else v + v_f
-            ubuf[c, x] = u
-            vbuf[c, x] = v
-        gbuf[x] = total
+            ubuf[c, x] = place(u)
+            vbuf[c, x] = place(v)
+        gbuf[x] = place(total)
         return carry
 
     for q in range(QUARTERS):
         for load in dft_loads[q]:
             load.wait()
         lax.fori_loop(q * rows, (q + 1) * rows, dft_plane, 0)
-
     loads[6].wait()
-    for copy in second:
-        copy.wait()
+
+    half_low = jnp.where(low, COURANT, 0.0)
+    sent_z.wait()
+    sent_xz.wait()
+    sent_yz.wait()
+    z_recv = zf[...]
+    xz_recv = xz[...]
+    z_sign = jnp.where(lax.rem(lax.div(lane, nx), 2) == 0, COURANT, -COURANT)
+    z_below = z_recv + z_sign * first_e + COURANT * xz_recv
+    z_below = z_below - jnp.where(row == ny - 1, COURANT * yz[nx : nx + 1, :], 0.0)
+    z_below = jnp.where(low, 0.0, z_below)
+    z_above = jnp.where(low, z_sign * z_recv, 0.0)
+
+    def z_plane(x, carry):
+        for r in range(2):
+            for c in range(2):
+                k = (r * 2 + c) * nx + x
+                edge = pltpu.roll(z_above, nz - 1 - k, 1)
+                value = hbuf[r, c, x + 1, 8 : ny + 8, :]
+                hbuf[r, c, x + 1, 8 : ny + 8, :] = value + jnp.where(lane == nz - 1, edge, 0.0)
+        return carry
+
+    sent_xp.wait_send()
+
+    @pl.when(low)
+    def _():
+        lax.fori_loop(0, nx, z_plane, 0)
+
+    sent_ye.wait()
+    sent_yp.wait()
+    sent_xyb.wait()
     for r in range(2):
-        for i in range(2):
-            hbuf[r, 1 + i, 0, 8 : ny + 8, :] = xh2[r, i]
-            hbuf[r, 2 * i, 1 : nx + 1, 7, :] = yh2[r, i]
-
-    z_below = jnp.where(low, 0.0, zh2[...])
-    shift = slab * z_other
+        h0, h2 = hbuf[r, 0, 1 : nx + 1, ny + 7, :], hbuf[r, 2, 1 : nx + 1, ny + 7, :]
+        hbuf[r, 0, 1 : nx + 1, ny + 7, :] = h0 - COURANT * ye[r, 1]
+        hbuf[r, 2, 1 : nx + 1, ny + 7, :] = h2 + COURANT * ye[r, 0]
+        edge = pltpu.roll(yz[0:nx, :], nz - 1 - r, 1)
+        edge = jnp.where(lane_x == nz - 1, half_low * edge, 0.0)
+        hbuf[r, 0, 1 : nx + 1, 7, :] = yp[r, 0] - COURANT * ye_out[r, 1] + edge
+        corner = jnp.where(row_x == nx - 1, COURANT * xyb[r : r + 1, :], 0.0)
+        hbuf[r, 2, 1 : nx + 1, 7, :] = yp[r, 1] + COURANT * ye_out[r, 0] - corner
+    sent_xe.wait()
+    sent_xp.wait_recv()
+    sent_xya.wait()
+    for r in range(2):
+        hbuf[r, 1, nx, 8 : ny + 8, :] = hbuf[r, 1, nx, 8 : ny + 8, :] + COURANT * xe[r, 1]
+        hbuf[r, 2, nx, 8 : ny + 8, :] = hbuf[r, 2, nx, 8 : ny + 8, :] - COURANT * xe[r, 0]
+        k = r * 2 * nx + 2 * nx - 1
+        edge = jnp.where(lane == nz - 1, half_low * pltpu.roll(xz_recv, nz - 1 - k, 1), 0.0)
+        hbuf[r, 1, 0, 8 : ny + 8, :] = xp[r, 0] + COURANT * ebuf[r, 2, 0, 0:ny, :] - edge
+        corner = jnp.where(row == ny - 1, COURANT * xya[r : r + 1, :], 0.0)
+        hbuf[r, 2, 0, 8 : ny + 8, :] = xp[r, 1] - COURANT * ebuf[r, 1, 0, 0:ny, :] + corner
 
     def e_plane(x, carry):
         m = matb[x]
@@ -211,7 +291,7 @@
             for c, curl in enumerate((curl_x, curl_y, curl_z)):
                 new_e = ebuf[r, c, x, 0:ny, :] + coefficient * curl
                 ebuf[r, c, x, 0:ny, :] = new_e
-                fields.append(pltpu.roll(new_e, shift, 1)[:, 0:slab])
+                fields.append(new_e)
             cells.append(fields)
         total = gbuf[x]
         for c in range(3):
@@ -227,7 +307,7 @@
         precision=lax.Precision.HIGHEST, preferred_element_type=F32,
     )
     part_out[...] = jnp.where(low, sums[owned:LAYERS], sums[0:owned])
-    last = send(6, part_out, part_in, {"gz": z_other})
+    last = send(9, part_out, part_in, to_z)
     mine = jnp.where(low, sums[0:owned], sums[owned:LAYERS])
     last.wait()
     result = (mine + part_in[...]) / own_thickness
@@ -276,26 +356,32 @@
             pltpu.VMEM(da.shape, F32),
             pltpu.SMEM(freq.shape, F32),
             pltpu.VMEM(lmap.shape, jnp.int32),
-            pltpu.VMEM((comps, nx, ny, slab), F32),
-            pltpu.VMEM((comps, nx, ny, slab), F32),
-            pltpu.VMEM((nx, ny, slab), F32),
-            pltpu.VMEM((nx * ny, slab), F32),
+            pltpu.VMEM((comps, nx, ny, nz), F32),
+            pltpu.VMEM((comps, nx, ny, nz), F32),
+            pltpu.VMEM((nx, ny, nz), F32),
+            pltpu.VMEM((nx * ny, nz), F32),
+            pltpu.VMEM((2, 2, nx, nz), F32),
+            pltpu.VMEM((2, nz), F32),
+            pltpu.VMEM((2, nz), F32),
+            pltpu.VMEM((ny, nz), F32),
+            pltpu.VMEM((nx + 8, nz), F32),
             pltpu.VMEM((2, 2, nx, nz), F32),
             pltpu.VMEM((ny, nz), F32),
+            pltpu.VMEM((owned, nx * ny), F32),
             pltpu.VMEM((2, 2, ny, nz), F32),
             pltpu.VMEM((2, 2, nx, nz), F32),
+            pltpu.VMEM((2, nz), F32),
+            pltpu.VMEM((2, nz), F32),
             pltpu.VMEM((ny, nz), F32),
-            pltpu.VMEM((2, 2, nx, nz), F32),
-            pltpu.VMEM((ny, nz), F32),
+            pltpu.VMEM((nx + 8, nz), F32),
             pltpu.VMEM((2, 2, ny, nz), F32),
             pltpu.VMEM((2, 2, nx, nz), F32),
             pltpu.VMEM((ny, nz), F32),
             pltpu.VMEM((owned, nx * ny), F32),
-            pltpu.VMEM((owned, nx * ny), F32),
             pltpu.SemaphoreType.DMA((7,)),
             pltpu.SemaphoreType.DMA((2, QUARTERS)),
-            pltpu.SemaphoreType.DMA((7,)),
-            pltpu.SemaphoreType.DMA((7,)),
+            pltpu.SemaphoreType.DMA((10,)),
+            pltpu.SemaphoreType.DMA((10,)),
         ],
         compiler_params=pltpu.CompilerParams(
             collective_id=0, has_side_effects=True, vmem_limit_bytes=24 << 20

time: 27.6 us -> 23.4 us (0.85)
  the two profiles are of different devices: /device:TPU:16 before, /device:TPU:15 now
where the time goes in v2:
time: 23.4 us; the launch traced here: 23.3 us
  Pallas kernels  22.6 us (97%)
  between operations  0.64 us (3%)
    pallas_call x1, Pallas kernels, shards(): pl.pallas_call(step_kernel, name='yee_step', out_shape=(pltpu.VMEM(padded...  20.9 us
    pallas_call x1, Pallas kernels, shards(): pl.pallas_call(store_kernel, name='store_fields', out_shape=(field, field...  1.71 us

profile of v2, /device:TPU:15, one launch (start us, length us, event | category | flops | bytes accessed | tf_op | source)
XLA Modules:
  0.0 23.3 jit_solution(16482274849340777521)
XLA Ops:
  0.6 20.9 %yee_step.1 = (f32[2,3,17,40,128]{4,3,2,1,0:T(8,128)S(1)}, f32[2,3,17,40,128]{4,3,2,1,0:T(8,128)S(1)}, f32[8,16,32]{2,1,0:T(8,128)S(1)}) custom-call(f32[3,16,32,128]{3,2,1,0:T(8,128)} %ef.1, f32[3,16,32,128]{3,2,1,0:T(8,128)} %hf.1, f32[3,16,32,128]{3,2,1,0:T(8,128)} %ea.1, f32[3,16,32,128]{3,2,1,0:T(8,128)} %ha.1, s32[16,32,128]{2,1,0:T(8,128)} %mat.1, ...), custom_call_target="tpu_custom_call" | custom-call | tf_op jit(solution)/shard_map/yee_step/pallas_call | solution.py:343
  21.6 1.7 %store_fields.1 = (f32[3,16,32,128]{3,2,1,0:T(8,128)}, f32[3,16,32,128]{3,2,1,0:T(8,128)}, f32[3,16,32,128]{3,2,1,0:T(8,128)}, f32[3,16,32,128]{3,2,1,0:T(8,128)}, f32[8,16,32]{2,1,0:T(8,128)}) custom-call(f32[2,3,17,40,128]{4,3,2,1,0:T(8,128)S(1)} %get-tuple-element.8.ebuf, f32[2,3,17,40,128]{4,3,2,1,0:T(8,128)S(1)} %get-tuple-element.9.hbuf, ...), custom_call_target="tpu_custom_call" | custom-call | tf_op jit(solution)/shard_map/store_fields/pallas_call | solution.py:392

commit v3 on v2

--- a/solution.py
+++ b/solution.py
@@ -17,7 +17,7 @@
 def step_kernel(
     ef, hf, ea, ha, mat, df, da, freq, lmap,
     ebuf, hbuf, grad,
-    matb, dfb, dab, freqb, lmapb, ubuf, vbuf, gbuf, prod,
+    matb, dfb, dab, freqb, lmapb, ubuf, vbuf, gbuf, prod, below,
     ye_out, xya_out, xyb_out, xz_out, yz_out, yp_out, z_out, part_out,
     xe, ye, xya, xyb, xz, yz, xp, yp, zf, part_in,
     lsem, dsem, ssem, rsem,
@@ -53,9 +53,10 @@
             pltpu.make_async_copy(df.at[:, :, :, part], dfb.at[:, :, :, part], dsem.at[0, q]),
             pltpu.make_async_copy(da.at[:, :, :, part], dab.at[:, :, :, part], dsem.at[1, q]),
         )
+        dft_loads.append(pair)
+    for pair in dft_loads[:2]:
         for load in pair:
             load.start()
-        dft_loads.append(pair)
 
     to_xe, to_xp = {"gx": x_down}, {"gx": x_up}
     to_ye, to_yp = {"gy": y_down}, {"gy": y_up}
@@ -72,24 +73,24 @@
     lane_x = lax.broadcasted_iota(jnp.int32, (nx, nz), 1)
     row_x = lax.broadcasted_iota(jnp.int32, (nx, nz), 0)
 
-    def send(index, src, dst, peer):
-        copy = pltpu.make_async_remote_copy(
+    def copy_to(index, src, dst, peer):
+        return pltpu.make_async_remote_copy(
             src_ref=src, dst_ref=dst, send_sem=ssem.at[index], recv_sem=rsem.at[index],
             device_id=peer, device_id_type=MESH,
         )
+
+    def send(index, src, dst, peer):
+        copy = copy_to(index, src, dst, peer)
         copy.start()
         return copy
 
     def gather_lane(tile_of, from_lane):
-        def body(x, acc):
-            for r in range(2):
-                for c in range(2):
-                    k = (r * 2 + c) * nx + x
-                    moved = pltpu.roll(tile_of(r, c, x), lax.rem(k - from_lane + nz, nz), 1)
-                    acc = jnp.where(lane == k, moved, acc)
-            return acc
-
-        return lax.fori_loop(0, nx, body, jnp.zeros((ny, nz), F32))
+        acc = jnp.zeros((ny, nz), F32)
+        for k in range(4 * nx):
+            tile = tile_of(k // (2 * nx), k // nx % 2, k % nx)
+            by = (k - from_lane) % nz
+            acc = jnp.where(lane == k, pltpu.roll(tile, by, 1) if by else tile, acc)
+        return acc
 
     loads[0].wait()
     loads[1].wait()
@@ -121,6 +122,14 @@
     sent_xe = send(3, ebuf.at[:, 1:3, 0, 0:ny, :], xe, to_xe)
     sent_xz = send(4, xz_out, xz, to_xz)
     sent_yz = send(5, yz_out, yz, to_yz)
+    sent_z = copy_to(8, z_out, zf, to_z)
+
+    @pl.when(jnp.logical_not(low))
+    def _():
+        z_out[...] = gather_lane(lambda r, c, x: ebuf[r, 1 - c, x, 0:ny, :], 0)
+        sent_z.start()
+
+    below[...] = jnp.zeros_like(below)
 
     zero_row = jnp.zeros((nx, nz), F32)
     for r in range(2):
@@ -162,10 +171,15 @@
         for i, c in enumerate((0, 2)):
             yp_out[r, i] = hbuf[r, c, 1 : nx + 1, ny + 7, :]
     sent_yp = send(7, yp_out, yp, to_yp)
-    first_e = gather_lane(lambda r, c, x: ebuf[r, 1 - c, x, 0:ny, :], 0)
-    last_h = gather_lane(lambda r, c, x: hbuf[r, c, x + 1, 8 : ny + 8, :], nz - 1)
-    z_out[...] = jnp.where(low, last_h, first_e)
-    sent_z = send(8, z_out, zf, to_z)
+
+    @pl.when(low)
+    def _():
+        z_out[...] = gather_lane(lambda r, c, x: hbuf[r, c, x + 1, 8 : ny + 8, :], nz - 1)
+        sent_z.start()
+
+    for pair in dft_loads[2:]:
+        for load in pair:
+            load.start()
 
     loads[4].wait()
     loads[5].wait()
@@ -219,28 +233,24 @@
     sent_z.wait()
     sent_xz.wait()
     sent_yz.wait()
-    z_recv = zf[...]
     xz_recv = xz[...]
     z_sign = jnp.where(lax.rem(lax.div(lane, nx), 2) == 0, COURANT, -COURANT)
-    z_below = z_recv + z_sign * first_e + COURANT * xz_recv
-    z_below = z_below - jnp.where(row == ny - 1, COURANT * yz[nx : nx + 1, :], 0.0)
-    z_below = jnp.where(low, 0.0, z_below)
-    z_above = jnp.where(low, z_sign * z_recv, 0.0)
-
-    def z_plane(x, carry):
-        for r in range(2):
-            for c in range(2):
-                k = (r * 2 + c) * nx + x
-                edge = pltpu.roll(z_above, nz - 1 - k, 1)
-                value = hbuf[r, c, x + 1, 8 : ny + 8, :]
-                hbuf[r, c, x + 1, 8 : ny + 8, :] = value + jnp.where(lane == nz - 1, edge, 0.0)
-        return carry
-
+    planes = [(r, c, x, (r * 2 + c) * nx + x) for r in range(2) for c in range(2) for x in range(nx)]
     sent_xp.wait_send()
 
     @pl.when(low)
     def _():
-        lax.fori_loop(0, nx, z_plane, 0)
+        z_above = z_sign * zf[...]
+        for r, c, x, k in planes:
+            edge = jnp.where(lane == nz - 1, pltpu.roll(z_above, nz - 1 - k, 1), 0.0)
+            hbuf[r, c, x + 1, 8 : ny + 8, :] = hbuf[r, c, x + 1, 8 : ny + 8, :] + edge
+
+    @pl.when(jnp.logical_not(low))
+    def _():
+        z_below = zf[...] + z_sign * z_out[...] + COURANT * xz_recv
+        z_below = z_below - jnp.where(row == ny - 1, COURANT * yz[nx : nx + 1, :], 0.0)
+        for r, c, x, k in planes:
+            below[r, c, x] = pltpu.roll(z_below, nz - k, 1) if k else z_below
 
     sent_ye.wait()
     sent_yp.wait()
@@ -280,9 +290,7 @@
             h2 = hbuf[r, 2, x + 1, 8 : ny + 8, :]
 
             def down_z(value, c):
-                k = (r * 2 + c) * nx + x
-                edge = pltpu.roll(z_below, lax.rem(nz - k, nz), 1)
-                return jnp.where(lane == 0, edge, pltpu.roll(value, 1, 1))
+                return jnp.where(lane == 0, below[r, c, x], pltpu.roll(value, 1, 1))
 
             curl_x = (h2 - hbuf[r, 2, x + 1, 7 : ny + 7, :]) - (h1 - down_z(h1, 1))
             curl_y = (h0 - down_z(h0, 0)) - (h2 - hbuf[r, 2, x, 8 : ny + 8, :])
@@ -360,6 +368,7 @@
             pltpu.VMEM((comps, nx, ny, nz), F32),
             pltpu.VMEM((nx, ny, nz), F32),
             pltpu.VMEM((nx * ny, nz), F32),
+            pltpu.VMEM((2, 2, nx, ny, nz), F32),
             pltpu.VMEM((2, 2, nx, nz), F32),
             pltpu.VMEM((2, nz), F32),
             pltpu.VMEM((2, nz), F32),

time: 23.4 us -> 21.6 us (0.923)
  the two profiles are of different devices: /device:TPU:15 before, /device:TPU:16 now
where the time goes in v3:
time: 21.6 us; the launch traced here: 21.3 us
  Pallas kernels  20.6 us (95%)
  between operations  0.64 us (3%)
    pallas_call x1, Pallas kernels, shards(): pl.pallas_call(step_kernel, name='yee_step', out_shape=(pltpu.VMEM(padded...  18.9 us
    pallas_call x1, Pallas kernels, shards(): pl.pallas_call(store_kernel, name='store_fields', out_shape=(field, field...  1.71 us

profile of v3, /device:TPU:16, one launch (start us, length us, event | category | flops | bytes accessed | tf_op | source)
XLA Modules:
  0.0 21.3 jit_solution(15495245980040869396)
XLA Ops:
  0.6 18.9 %yee_step.1 = (f32[2,3,17,40,128]{4,3,2,1,0:T(8,128)S(1)}, f32[2,3,17,40,128]{4,3,2,1,0:T(8,128)S(1)}, f32[8,16,32]{2,1,0:T(8,128)S(1)}) custom-call(f32[3,16,32,128]{3,2,1,0:T(8,128)} %ef.1, f32[3,16,32,128]{3,2,1,0:T(8,128)} %hf.1, f32[3,16,32,128]{3,2,1,0:T(8,128)} %ea.1, f32[3,16,32,128]{3,2,1,0:T(8,128)} %ha.1, s32[16,32,128]{2,1,0:T(8,128)} %mat.1, ...), custom_call_target="tpu_custom_call" | custom-call | tf_op jit(solution)/shard_map/yee_step/pallas_call | solution.py:351
  19.5 1.7 %store_fields.1 = (f32[3,16,32,128]{3,2,1,0:T(8,128)}, f32[3,16,32,128]{3,2,1,0:T(8,128)}, f32[3,16,32,128]{3,2,1,0:T(8,128)}, f32[3,16,32,128]{3,2,1,0:T(8,128)}, f32[8,16,32]{2,1,0:T(8,128)}) custom-call(f32[2,3,17,40,128]{4,3,2,1,0:T(8,128)S(1)} %get-tuple-element.8.ebuf, f32[2,3,17,40,128]{4,3,2,1,0:T(8,128)S(1)} %get-tuple-element.9.hbuf, ...), custom_call_target="tpu_custom_call" | custom-call | tf_op jit(solution)/shard_map/store_fields/pallas_call | solution.py:401

commit v4 on v3

--- a/solution.py
+++ b/solution.py
@@ -33,6 +33,16 @@
     low = gz == 0
     x_cross = lax.rem(gx + sx + 2 * gz - 1, sx)
     y_cross = lax.rem(gy + sy + 2 * gz - 1, sy)
+
+    to_xe, to_xp = {"gx": x_down}, {"gx": x_up}
+    to_ye, to_yp = {"gy": y_down}, {"gy": y_up}
+    to_z = {"gz": z_other}
+    to_xya, to_xyb = {"gx": x_up, "gy": y_down}, {"gx": x_down, "gy": y_up}
+    to_xz, to_yz = {"gx": x_cross, "gz": z_other}, {"gy": y_cross, "gz": z_other}
+    peers = (to_xe, to_xp, to_ye, to_yp, to_z, to_xya, to_xyb, to_xz, to_yz)
+    barrier = pltpu.get_barrier_semaphore()
+    for peer in peers:
+        pl.semaphore_signal(barrier, inc=1, device_id=peer, device_id_type=MESH)
 
     loads = [
         pltpu.make_async_copy(ef, ebuf.at[0, :, 0:nx, 0:ny, :], lsem.at[0]),
@@ -58,16 +68,6 @@
         for load in pair:
             load.start()
 
-    to_xe, to_xp = {"gx": x_down}, {"gx": x_up}
-    to_ye, to_yp = {"gy": y_down}, {"gy": y_up}
-    to_z = {"gz": z_other}
-    to_xya, to_xyb = {"gx": x_up, "gy": y_down}, {"gx": x_down, "gy": y_up}
-    to_xz, to_yz = {"gx": x_cross, "gz": z_other}, {"gy": y_cross, "gz": z_other}
-    peers = (to_xe, to_xp, to_ye, to_yp, to_z, to_xya, to_xyb, to_xz, to_yz)
-    barrier = pltpu.get_barrier_semaphore()
-    for peer in peers:
-        pl.semaphore_signal(barrier, inc=1, device_id=peer, device_id_type=MESH)
-
     lane = lax.broadcasted_iota(jnp.int32, (ny, nz), 1)
     row = lax.broadcasted_iota(jnp.int32, (ny, nz), 0)
     lane_x = lax.broadcasted_iota(jnp.int32, (nx, nz), 1)
@@ -115,21 +115,11 @@
     xz_out[...] = xz_tile
     yz_out[0:nx, :] = yz_tile
     yz_out[nx : nx + 8, :] = jnp.broadcast_to(yz_row, (8, nz))
-    pl.semaphore_wait(barrier, len(peers))
-    sent_xya = send(0, xya_out, xya, to_xya)
-    sent_xyb = send(1, xyb_out, xyb, to_xyb)
-    sent_ye = send(2, ye_out, ye, to_ye)
-    sent_xe = send(3, ebuf.at[:, 1:3, 0, 0:ny, :], xe, to_xe)
-    sent_xz = send(4, xz_out, xz, to_xz)
-    sent_yz = send(5, yz_out, yz, to_yz)
-    sent_z = copy_to(8, z_out, zf, to_z)
 
     @pl.when(jnp.logical_not(low))
     def _():
         z_out[...] = gather_lane(lambda r, c, x: ebuf[r, 1 - c, x, 0:ny, :], 0)
-        sent_z.start()
-
-    below[...] = jnp.zeros_like(below)
+
 
     zero_row = jnp.zeros((nx, nz), F32)
     for r in range(2):
@@ -160,23 +150,31 @@
                 hbuf[r, c, x + 1, 8 : ny + 8, :] = hbuf[r, c, x + 1, 8 : ny + 8, :] - COURANT * curl
 
     h_plane(nx - 1, last=True)
-    sent_xp = send(6, hbuf.at[:, 1:3, nx, 8 : ny + 8, :], xp, to_xp)
 
     def h_body(x, carry):
         h_plane(x)
         return carry
 
-    lax.fori_loop(0, nx - 1, h_body, 0)
+    lax.fori_loop(0, nx - 1, h_body, 0, unroll=3)
     for r in range(2):
         for i, c in enumerate((0, 2)):
             yp_out[r, i] = hbuf[r, c, 1 : nx + 1, ny + 7, :]
-    sent_yp = send(7, yp_out, yp, to_yp)
 
     @pl.when(low)
     def _():
         z_out[...] = gather_lane(lambda r, c, x: hbuf[r, c, x + 1, 8 : ny + 8, :], nz - 1)
-        sent_z.start()
-
+
+    pl.semaphore_wait(barrier, len(peers))
+    sent_xe = send(3, ebuf.at[:, 1:3, 0, 0:ny, :], xe, to_xe)
+    sent_xz = send(4, xz_out, xz, to_xz)
+    sent_xya = send(0, xya_out, xya, to_xya)
+    sent_xyb = send(1, xyb_out, xyb, to_xyb)
+    sent_z = send(8, z_out, zf, to_z)
+    sent_yp = send(7, yp_out, yp, to_yp)
+    sent_ye = send(2, ye_out, ye, to_ye)
+    sent_xp = send(6, hbuf.at[:, 1:3, nx, 8 : ny + 8, :], xp, to_xp)
+    sent_yz = send(5, yz_out, yz, to_yz)
+    below[...] = jnp.zeros_like(below)
     for pair in dft_loads[2:]:
         for load in pair:
             load.start()
@@ -226,7 +224,7 @@
     for q in range(QUARTERS):
         for load in dft_loads[q]:
             load.wait()
-        lax.fori_loop(q * rows, (q + 1) * rows, dft_plane, 0)
+        lax.fori_loop(q * rows, (q + 1) * rows, dft_plane, 0, unroll=2)
     loads[6].wait()
 
     half_low = jnp.where(low, COURANT, 0.0)
@@ -308,7 +306,7 @@
         prod[pl.ds(pl.multiple_of(x * ny, ny), ny), :] = total
         return carry
 
-    lax.fori_loop(0, nx, e_plane, 0)
+    lax.fori_loop(0, nx, e_plane, 0, unroll=2)
 
     sums = lax.dot_general(
         onehot, prod[...], (((1,), (1,)), ((), ())),

time: 21.6 us -> 20.5 us (0.949); the launches traced: 21.3 us -> 20.4 us
  Pallas kernels: 20.6 us -> 19.8 us
    pallas_call x1, Pallas kernels: 18.9 us -> 18.1 us  [shards(): pl.pallas_call(step_kernel, name='yee_step', out_shape=(pltpu.VMEM(padded...]
where the time goes in v4:
time: 20.5 us; the launch traced here: 20.4 us
  Pallas kernels  19.8 us (97%)
  between operations  0.64 us (3%)
    pallas_call x1, Pallas kernels, shards(): pl.pallas_call(step_kernel, name='yee_step', out_shape=(pltpu.VMEM(padded...  18.1 us
    pallas_call x1, Pallas kernels, shards(): pl.pallas_call(store_kernel, name='store_fields', out_shape=(field, field...  1.71 us

profile of v4, /device:TPU:16, one launch (start us, length us, event | category | flops | bytes accessed | tf_op | source)
XLA Modules:
  0.0 20.4 jit_solution(15981571787423306242)
XLA Ops:
  0.6 18.1 %yee_step.1 = (f32[2,3,17,40,128]{4,3,2,1,0:T(8,128)S(1)}, f32[2,3,17,40,128]{4,3,2,1,0:T(8,128)S(1)}, f32[8,16,32]{2,1,0:T(8,128)S(1)}) custom-call(f32[3,16,32,128]{3,2,1,0:T(8,128)} %ef.1, f32[3,16,32,128]{3,2,1,0:T(8,128)} %hf.1, f32[3,16,32,128]{3,2,1,0:T(8,128)} %ea.1, f32[3,16,32,128]{3,2,1,0:T(8,128)} %ha.1, s32[16,32,128]{2,1,0:T(8,128)} %mat.1, ...), custom_call_target="tpu_custom_call" | custom-call | tf_op jit(solution)/shard_map/yee_step/pallas_call | solution.py:349
  18.7 1.7 %store_fields.1 = (f32[3,16,32,128]{3,2,1,0:T(8,128)}, f32[3,16,32,128]{3,2,1,0:T(8,128)}, f32[3,16,32,128]{3,2,1,0:T(8,128)}, f32[3,16,32,128]{3,2,1,0:T(8,128)}, f32[8,16,32]{2,1,0:T(8,128)}) custom-call(f32[2,3,17,40,128]{4,3,2,1,0:T(8,128)S(1)} %get-tuple-element.8.ebuf, f32[2,3,17,40,128]{4,3,2,1,0:T(8,128)S(1)} %get-tuple-element.9.hbuf, ...), custom_call_target="tpu_custom_call" | custom-call | tf_op jit(solution)/shard_map/store_fields/pallas_call | solution.py:399

commit v5 on v4

--- a/solution.py
+++ b/solution.py
@@ -20,7 +20,7 @@
     matb, dfb, dab, freqb, lmapb, ubuf, vbuf, gbuf, prod, below,
     ye_out, xya_out, xyb_out, xz_out, yz_out, yp_out, z_out, part_out,
     xe, ye, xya, xyb, xz, yz, xp, yp, zf, part_in,
-    lsem, dsem, ssem, rsem,
+    fsem, lsem, dsem, ssem, rsem,
 ):
     nx, ny, nz = mat.shape
     freqs, slab = df.shape[0], df.shape[5]
@@ -44,18 +44,26 @@
     for peer in peers:
         pl.semaphore_signal(barrier, inc=1, device_id=peer, device_id_type=MESH)
 
+    rows = nx // QUARTERS
+    field_loads = []
+    for q in reversed(range(QUARTERS)):
+        part, inner = pl.ds(q * rows, rows), pl.ds(q * rows + 1, rows)
+        group = [
+            pltpu.make_async_copy(ef.at[:, part], ebuf.at[0, :, part, 0:ny, :], fsem.at[0, q]),
+            pltpu.make_async_copy(ea.at[:, part], ebuf.at[1, :, part, 0:ny, :], fsem.at[1, q]),
+            pltpu.make_async_copy(hf.at[:, part], hbuf.at[0, :, inner, 8 : ny + 8, :], fsem.at[2, q]),
+            pltpu.make_async_copy(ha.at[:, part], hbuf.at[1, :, inner, 8 : ny + 8, :], fsem.at[3, q]),
+        ]
+        for load in group:
+            load.start()
+        field_loads.append((q, group))
     loads = [
-        pltpu.make_async_copy(ef, ebuf.at[0, :, 0:nx, 0:ny, :], lsem.at[0]),
-        pltpu.make_async_copy(ea, ebuf.at[1, :, 0:nx, 0:ny, :], lsem.at[1]),
-        pltpu.make_async_copy(hf, hbuf.at[0, :, 1 : nx + 1, 8 : ny + 8, :], lsem.at[2]),
-        pltpu.make_async_copy(ha, hbuf.at[1, :, 1 : nx + 1, 8 : ny + 8, :], lsem.at[3]),
-        pltpu.make_async_copy(freq, freqb, lsem.at[4]),
-        pltpu.make_async_copy(lmap, lmapb, lsem.at[5]),
-        pltpu.make_async_copy(mat, matb, lsem.at[6]),
+        pltpu.make_async_copy(freq, freqb, lsem.at[0]),
+        pltpu.make_async_copy(lmap, lmapb, lsem.at[1]),
+        pltpu.make_async_copy(mat, matb, lsem.at[2]),
     ]
     for load in loads:
         load.start()
-    rows = nx // QUARTERS
     dft_loads = []
     for q in range(QUARTERS):
         part = pl.ds(q * rows, rows)
@@ -84,16 +92,65 @@
         copy.start()
         return copy
 
-    def gather_lane(tile_of, from_lane):
-        acc = jnp.zeros((ny, nz), F32)
+    def gather_lane(tile_of, from_lane, first):
+        acc = z_out[...]
         for k in range(4 * nx):
-            tile = tile_of(k // (2 * nx), k // nx % 2, k % nx)
-            by = (k - from_lane) % nz
-            acc = jnp.where(lane == k, pltpu.roll(tile, by, 1) if by else tile, acc)
-        return acc
-
-    loads[0].wait()
-    loads[1].wait()
+            if first <= k % nx < first + rows:
+                tile = tile_of(k // (2 * nx), k // nx % 2, k % nx)
+                by = (k - from_lane) % nz
+                acc = jnp.where(lane == k, pltpu.roll(tile, by, 1) if by else tile, acc)
+        z_out[...] = acc
+
+    zero_row = jnp.zeros((nx, nz), F32)
+    for r in range(2):
+        ebuf[r, 0, 0:nx, ny, :] = zero_row
+        ebuf[r, 2, 0:nx, ny, :] = zero_row
+    z_out[...] = jnp.zeros_like(z_out)
+
+    def h_plane(x, last=False):
+        for r in range(2):
+            e0 = ebuf[r, 0, x, 0:ny, :]
+            e1 = ebuf[r, 1, x, 0:ny, :]
+            e2 = ebuf[r, 2, x, 0:ny, :]
+
+            def up_z(value):
+                return jnp.where(lane == nz - 1, 0.0, pltpu.roll(value, nz - 1, 1))
+
+            curl_x = (ebuf[r, 2, x, 1 : ny + 1, :] - e2) - (up_z(e1) - e1)
+            curl_y = up_z(e0) - e0
+            curl_z = ebuf[r, 0, x, 1 : ny + 1, :] - e0
+            if last:
+                curl_y = curl_y + e2
+                curl_z = -e1 - curl_z
+            else:
+                curl_y = curl_y - (ebuf[r, 2, x + 1, 0:ny, :] - e2)
+                curl_z = (ebuf[r, 1, x + 1, 0:ny, :] - e1) - curl_z
+            for c, curl in enumerate((curl_x, curl_y, curl_z)):
+                hbuf[r, c, x + 1, 8 : ny + 8, :] = hbuf[r, c, x + 1, 8 : ny + 8, :] - COURANT * curl
+
+    def h_body(x, carry):
+        h_plane(x)
+        return carry
+
+    for q, group in field_loads:
+        for load in group:
+            load.wait()
+        if q == QUARTERS - 1:
+            h_plane(nx - 1, last=True)
+        lax.fori_loop(q * rows, min((q + 1) * rows, nx - 1), h_body, 0, unroll=True)
+
+        @pl.when(low)
+        def _():
+            gather_lane(lambda r, c, x: hbuf[r, c, x + 1, 8 : ny + 8, :], nz - 1, q * rows)
+
+        @pl.when(jnp.logical_not(low))
+        def _():
+            gather_lane(lambda r, c, x: ebuf[r, 1 - c, x, 0:ny, :], 0, q * rows)
+
+    for r in range(2):
+        for i, c in enumerate((0, 2)):
+            yp_out[r, i] = hbuf[r, c, 1 : nx + 1, ny + 7, :]
+
     xz_tile = jnp.zeros((ny, nz), F32)
     yz_tile = jnp.zeros((nx, nz), F32)
     yz_row = jnp.zeros((1, nz), F32)
@@ -116,71 +173,22 @@
     yz_out[0:nx, :] = yz_tile
     yz_out[nx : nx + 8, :] = jnp.broadcast_to(yz_row, (8, nz))
 
-    @pl.when(jnp.logical_not(low))
-    def _():
-        z_out[...] = gather_lane(lambda r, c, x: ebuf[r, 1 - c, x, 0:ny, :], 0)
-
-
-    zero_row = jnp.zeros((nx, nz), F32)
-    for r in range(2):
-        ebuf[r, 0, 0:nx, ny, :] = zero_row
-        ebuf[r, 2, 0:nx, ny, :] = zero_row
-    loads[2].wait()
-    loads[3].wait()
-
-    def h_plane(x, last=False):
-        for r in range(2):
-            e0 = ebuf[r, 0, x, 0:ny, :]
-            e1 = ebuf[r, 1, x, 0:ny, :]
-            e2 = ebuf[r, 2, x, 0:ny, :]
-
-            def up_z(value):
-                return jnp.where(lane == nz - 1, 0.0, pltpu.roll(value, nz - 1, 1))
-
-            curl_x = (ebuf[r, 2, x, 1 : ny + 1, :] - e2) - (up_z(e1) - e1)
-            curl_y = up_z(e0) - e0
-            curl_z = ebuf[r, 0, x, 1 : ny + 1, :] - e0
-            if last:
-                curl_y = curl_y + e2
-                curl_z = -e1 - curl_z
-            else:
-                curl_y = curl_y - (ebuf[r, 2, x + 1, 0:ny, :] - e2)
-                curl_z = (ebuf[r, 1, x + 1, 0:ny, :] - e1) - curl_z
-            for c, curl in enumerate((curl_x, curl_y, curl_z)):
-                hbuf[r, c, x + 1, 8 : ny + 8, :] = hbuf[r, c, x + 1, 8 : ny + 8, :] - COURANT * curl
-
-    h_plane(nx - 1, last=True)
-
-    def h_body(x, carry):
-        h_plane(x)
-        return carry
-
-    lax.fori_loop(0, nx - 1, h_body, 0, unroll=3)
-    for r in range(2):
-        for i, c in enumerate((0, 2)):
-            yp_out[r, i] = hbuf[r, c, 1 : nx + 1, ny + 7, :]
-
-    @pl.when(low)
-    def _():
-        z_out[...] = gather_lane(lambda r, c, x: hbuf[r, c, x + 1, 8 : ny + 8, :], nz - 1)
-
     pl.semaphore_wait(barrier, len(peers))
-    sent_xe = send(3, ebuf.at[:, 1:3, 0, 0:ny, :], xe, to_xe)
-    sent_xz = send(4, xz_out, xz, to_xz)
     sent_xya = send(0, xya_out, xya, to_xya)
     sent_xyb = send(1, xyb_out, xyb, to_xyb)
+    sent_xz = send(4, xz_out, xz, to_xz)
+    sent_yz = send(5, yz_out, yz, to_yz)
     sent_z = send(8, z_out, zf, to_z)
     sent_yp = send(7, yp_out, yp, to_yp)
     sent_ye = send(2, ye_out, ye, to_ye)
     sent_xp = send(6, hbuf.at[:, 1:3, nx, 8 : ny + 8, :], xp, to_xp)
-    sent_yz = send(5, yz_out, yz, to_yz)
-    below[...] = jnp.zeros_like(below)
+    sent_xe = send(3, ebuf.at[:, 1:3, 0, 0:ny, :], xe, to_xe)
     for pair in dft_loads[2:]:
         for load in pair:
             load.start()
-
-    loads[4].wait()
-    loads[5].wait()
+    below[...] = jnp.zeros_like(below)
+    loads[0].wait()
+    loads[1].wait()
     cosine, sine = [], []
     squares = None
     for f in range(freqs):
@@ -225,54 +233,43 @@
         for load in dft_loads[q]:
             load.wait()
         lax.fori_loop(q * rows, (q + 1) * rows, dft_plane, 0, unroll=2)
-    loads[6].wait()
+    loads[2].wait()
 
     half_low = jnp.where(low, COURANT, 0.0)
+    half_high = COURANT - half_low
     sent_z.wait()
-    sent_xz.wait()
     sent_yz.wait()
-    xz_recv = xz[...]
     z_sign = jnp.where(lax.rem(lax.div(lane, nx), 2) == 0, COURANT, -COURANT)
-    planes = [(r, c, x, (r * 2 + c) * nx + x) for r in range(2) for c in range(2) for x in range(nx)]
-    sent_xp.wait_send()
+    places = [(r, c, x, (r * 2 + c) * nx + x) for r in range(2) for c in range(2) for x in range(nx)]
+    last_x = nx - 1
+
+    def add_above(r, c, x, k):
+        edge = jnp.where(lane == nz - 1, pltpu.roll(z_sign * zf[...], nz - 1 - k, 1), 0.0)
+        hbuf[r, c, x + 1, 8 : ny + 8, :] = hbuf[r, c, x + 1, 8 : ny + 8, :] + edge
 
     @pl.when(low)
     def _():
-        z_above = z_sign * zf[...]
-        for r, c, x, k in planes:
-            edge = jnp.where(lane == nz - 1, pltpu.roll(z_above, nz - 1 - k, 1), 0.0)
-            hbuf[r, c, x + 1, 8 : ny + 8, :] = hbuf[r, c, x + 1, 8 : ny + 8, :] + edge
+        for r, c, x, k in places:
+            if x < last_x:
+                add_above(r, c, x, k)
 
     @pl.when(jnp.logical_not(low))
     def _():
-        z_below = zf[...] + z_sign * z_out[...] + COURANT * xz_recv
+        z_below = zf[...] + z_sign * z_out[...]
         z_below = z_below - jnp.where(row == ny - 1, COURANT * yz[nx : nx + 1, :], 0.0)
-        for r, c, x, k in planes:
+        for r, c, x, k in places:
             below[r, c, x] = pltpu.roll(z_below, nz - k, 1) if k else z_below
 
     sent_ye.wait()
     sent_yp.wait()
-    sent_xyb.wait()
     for r in range(2):
-        h0, h2 = hbuf[r, 0, 1 : nx + 1, ny + 7, :], hbuf[r, 2, 1 : nx + 1, ny + 7, :]
-        hbuf[r, 0, 1 : nx + 1, ny + 7, :] = h0 - COURANT * ye[r, 1]
-        hbuf[r, 2, 1 : nx + 1, ny + 7, :] = h2 + COURANT * ye[r, 0]
+        h0, h2 = hbuf[r, 0, 1:nx, ny + 7, :], hbuf[r, 2, 1:nx, ny + 7, :]
+        hbuf[r, 0, 1:nx, ny + 7, :] = h0 - COURANT * ye[r, 1, 0:last_x]
+        hbuf[r, 2, 1:nx, ny + 7, :] = h2 + COURANT * ye[r, 0, 0:last_x]
         edge = pltpu.roll(yz[0:nx, :], nz - 1 - r, 1)
         edge = jnp.where(lane_x == nz - 1, half_low * edge, 0.0)
         hbuf[r, 0, 1 : nx + 1, 7, :] = yp[r, 0] - COURANT * ye_out[r, 1] + edge
-        corner = jnp.where(row_x == nx - 1, COURANT * xyb[r : r + 1, :], 0.0)
-        hbuf[r, 2, 1 : nx + 1, 7, :] = yp[r, 1] + COURANT * ye_out[r, 0] - corner
-    sent_xe.wait()
-    sent_xp.wait_recv()
-    sent_xya.wait()
-    for r in range(2):
-        hbuf[r, 1, nx, 8 : ny + 8, :] = hbuf[r, 1, nx, 8 : ny + 8, :] + COURANT * xe[r, 1]
-        hbuf[r, 2, nx, 8 : ny + 8, :] = hbuf[r, 2, nx, 8 : ny + 8, :] - COURANT * xe[r, 0]
-        k = r * 2 * nx + 2 * nx - 1
-        edge = jnp.where(lane == nz - 1, half_low * pltpu.roll(xz_recv, nz - 1 - k, 1), 0.0)
-        hbuf[r, 1, 0, 8 : ny + 8, :] = xp[r, 0] + COURANT * ebuf[r, 2, 0, 0:ny, :] - edge
-        corner = jnp.where(row == ny - 1, COURANT * xya[r : r + 1, :], 0.0)
-        hbuf[r, 2, 0, 8 : ny + 8, :] = xp[r, 1] - COURANT * ebuf[r, 1, 0, 0:ny, :] + corner
+        hbuf[r, 2, 1 : nx + 1, 7, :] = yp[r, 1] + COURANT * ye_out[r, 0]
 
     def e_plane(x, carry):
         m = matb[x]
@@ -303,10 +300,40 @@
         for c in range(3):
             fwd, adj = cells[0][c], cells[1][c]
             total = total + (fwd * (ubuf[c, x] + squares * adj) + adj * vbuf[c, x])
-        prod[pl.ds(pl.multiple_of(x * ny, ny), ny), :] = total
+        prod[pl.ds(pl.multiple_of(x * ny, ny) if not isinstance(x, int) else x * ny, ny), :] = total
         return carry
 
-    lax.fori_loop(0, nx, e_plane, 0, unroll=2)
+    lax.fori_loop(1, last_x, e_plane, 0, unroll=2)
+
+    sent_xe.wait()
+    sent_xp.wait()
+    sent_xz.wait()
+    sent_xya.wait()
+    sent_xyb.wait()
+
+    @pl.when(low)
+    def _():
+        for r, c, x, k in places:
+            if x == last_x:
+                add_above(r, c, x, k)
+
+    for r in range(2):
+        row_0, row_2 = hbuf[r, 0, nx, ny + 7 : ny + 8, :], hbuf[r, 2, nx, ny + 7 : ny + 8, :]
+        hbuf[r, 0, nx, ny + 7 : ny + 8, :] = row_0 - COURANT * ye[r, 1, last_x:nx, :]
+        hbuf[r, 2, nx, ny + 7 : ny + 8, :] = row_2 + COURANT * ye[r, 0, last_x:nx, :]
+        hbuf[r, 2, nx, 7:8, :] = hbuf[r, 2, nx, 7:8, :] - COURANT * xyb[r : r + 1, :]
+        hbuf[r, 1, nx, 8 : ny + 8, :] = hbuf[r, 1, nx, 8 : ny + 8, :] + COURANT * xe[r, 1]
+        hbuf[r, 2, nx, 8 : ny + 8, :] = hbuf[r, 2, nx, 8 : ny + 8, :] - COURANT * xe[r, 0]
+        k = r * 2 * nx + 2 * nx - 1
+        column = pltpu.roll(xz[...], nz - k, 1)
+        below[r, 1, last_x] = below[r, 1, last_x] + half_high * column
+        edge = jnp.where(lane == nz - 1, half_low * pltpu.roll(column, nz - 1, 1), 0.0)
+        hbuf[r, 1, 0, 8 : ny + 8, :] = xp[r, 0] + COURANT * ebuf[r, 2, 0, 0:ny, :] - edge
+        corner = jnp.where(row == ny - 1, COURANT * xya[r : r + 1, :], 0.0)
+        hbuf[r, 2, 0, 8 : ny + 8, :] = xp[r, 1] - COURANT * ebuf[r, 1, 0, 0:ny, :] + corner
+
+    e_plane(0, 0)
+    e_plane(last_x, 0)
 
     sums = lax.dot_general(
         onehot, prod[...], (((1,), (1,)), ((), ())),
@@ -385,7 +412,8 @@
             pltpu.VMEM((2, 2, nx, nz), F32),
             pltpu.VMEM((ny, nz), F32),
             pltpu.VMEM((owned, nx * ny), F32),
-            pltpu.SemaphoreType.DMA((7,)),
+            pltpu.SemaphoreType.DMA((4, QUARTERS)),
+            pltpu.SemaphoreType.DMA((3,)),
             pltpu.SemaphoreType.DMA((2, QUARTERS)),
             pltpu.SemaphoreType.DMA((10,)),
             pltpu.SemaphoreType.DMA((10,)),

time: 20.5 us -> 19.8 us (0.966); the launches traced: 20.4 us -> 19.5 us
  Pallas kernels: 19.8 us -> 18.9 us
    pallas_call x1, Pallas kernels: 18.1 us -> 17.1 us  [shards(): pl.pallas_call(step_kernel, name='yee_step', out_shape=(pltpu.VMEM(padded...]
where the time goes in v5:
time: 19.8 us; the launch traced here: 19.5 us
  Pallas kernels  18.9 us (95%)
  between operations  0.64 us (3%)
    pallas_call x1, Pallas kernels, shards(): pl.pallas_call(step_kernel, name='yee_step', out_shape=(pltpu.VMEM(padded...  17.1 us
    pallas_call x1, Pallas kernels, shards(): pl.pallas_call(store_kernel, name='store_fields', out_shape=(field, field...  1.71 us

profile of v5, /device:TPU:16, one launch (start us, length us, event | category | flops | bytes accessed | tf_op | source)
XLA Modules:
  0.0 19.5 jit_solution(8467089814473963661)
XLA Ops:
  0.6 17.1 %yee_step.1 = (f32[2,3,17,40,128]{4,3,2,1,0:T(8,128)S(1)}, f32[2,3,17,40,128]{4,3,2,1,0:T(8,128)S(1)}, f32[8,16,32]{2,1,0:T(8,128)S(1)}) custom-call(f32[3,16,32,128]{3,2,1,0:T(8,128)} %ef.1, f32[3,16,32,128]{3,2,1,0:T(8,128)} %hf.1, f32[3,16,32,128]{3,2,1,0:T(8,128)} %ea.1, f32[3,16,32,128]{3,2,1,0:T(8,128)} %ha.1, s32[16,32,128]{2,1,0:T(8,128)} %mat.1, ...), custom_call_target="tpu_custom_call" | custom-call | tf_op jit(solution)/shard_map/yee_step/pallas_call | solution.py:376
  17.8 1.7 %store_fields.1 = (f32[3,16,32,128]{3,2,1,0:T(8,128)}, f32[3,16,32,128]{3,2,1,0:T(8,128)}, f32[3,16,32,128]{3,2,1,0:T(8,128)}, f32[3,16,32,128]{3,2,1,0:T(8,128)}, f32[8,16,32]{2,1,0:T(8,128)}) custom-call(f32[2,3,17,40,128]{4,3,2,1,0:T(8,128)S(1)} %get-tuple-element.8.ebuf, f32[2,3,17,40,128]{4,3,2,1,0:T(8,128)S(1)} %get-tuple-element.9.hbuf, ...), custom_call_target="tpu_custom_call" | custom-call | tf_op jit(solution)/shard_map/store_fields/pallas_call | solution.py:427

commit v6 on v5

--- a/solution.py
+++ b/solution.py
@@ -238,7 +238,6 @@
     half_low = jnp.where(low, COURANT, 0.0)
     half_high = COURANT - half_low
     sent_z.wait()
-    sent_yz.wait()
     z_sign = jnp.where(lax.rem(lax.div(lane, nx), 2) == 0, COURANT, -COURANT)
     places = [(r, c, x, (r * 2 + c) * nx + x) for r in range(2) for c in range(2) for x in range(nx)]
     last_x = nx - 1
@@ -256,12 +255,70 @@
     @pl.when(jnp.logical_not(low))
     def _():
         z_below = zf[...] + z_sign * z_out[...]
-        z_below = z_below - jnp.where(row == ny - 1, COURANT * yz[nx : nx + 1, :], 0.0)
         for r, c, x, k in places:
             below[r, c, x] = pltpu.roll(z_below, nz - k, 1) if k else z_below
 
+    def e_rows(x, y0, n):
+        own, ahead = pl.ds(y0 + 8, n), pl.ds(y0 + 7, n)
+        cell = pl.ds(y0, n)
+        first_lane = lane[0:n] == 0
+        m = matb[x, cell]
+        coefficient = jnp.where(
+            m == 0, COURANT / PERMITTIVITIES[0],
+            jnp.where(m == 1, COURANT / PERMITTIVITIES[1],
+                      jnp.where(m == 2, COURANT / PERMITTIVITIES[2], COURANT / PERMITTIVITIES[3])),
+        ).astype(F32)
+        cells = []
+        for r in range(2):
+            h0 = hbuf[r, 0, x + 1, own, :]
+            h1 = hbuf[r, 1, x + 1, own, :]
+            h2 = hbuf[r, 2, x + 1, own, :]
+
+            def down_z(value, c):
+                return jnp.where(first_lane, below[r, c, x, cell], pltpu.roll(value, 1, 1))
+
+            curl_x = (h2 - hbuf[r, 2, x + 1, ahead, :]) - (h1 - down_z(h1, 1))
+            curl_y = (h0 - down_z(h0, 0)) - (h2 - hbuf[r, 2, x, own, :])
+            curl_z = (h1 - hbuf[r, 1, x, own, :]) - (h0 - hbuf[r, 0, x + 1, ahead, :])
+            fields = []
+            for c, curl in enumerate((curl_x, curl_y, curl_z)):
+                new_e = ebuf[r, c, x, cell, :] + coefficient * curl
+                ebuf[r, c, x, cell, :] = new_e
+                fields.append(new_e)
+            cells.append(fields)
+        total = gbuf[x, cell]
+        for c in range(3):
+            fwd, adj = cells[0][c], cells[1][c]
+            total = total + (fwd * (ubuf[c, x, cell] + squares * adj) + adj * vbuf[c, x, cell])
+        start = x * ny + y0
+        prod[pl.ds(start if isinstance(x, int) else pl.multiple_of(start, 8), n), :] = total
+
+    half = ny // 2
+
+    def middle_rows(x, carry):
+        e_rows(x, ny // 4, half)
+        return carry
+
+    def outer_rows(x, carry):
+        e_rows(x, 0, ny // 4)
+        e_rows(x, ny - ny // 4, ny // 4)
+        return carry
+
+    lax.fori_loop(1, last_x, middle_rows, 0, unroll=2)
+
+    sent_yz.wait()
     sent_ye.wait()
     sent_yp.wait()
+
+    @pl.when(jnp.logical_not(low))
+    def _():
+        bottom = lax.broadcasted_iota(jnp.int32, (8, nz), 0) == 7
+        missing = jnp.where(bottom, COURANT * yz[nx : nx + 8, :], 0.0)
+        for r, c, x, k in places:
+            if c == 0:
+                edge = pltpu.roll(missing, nz - k, 1) if k else missing
+                below[r, 0, x, ny - 8 : ny, :] = below[r, 0, x, ny - 8 : ny, :] - edge
+
     for r in range(2):
         h0, h2 = hbuf[r, 0, 1:nx, ny + 7, :], hbuf[r, 2, 1:nx, ny + 7, :]
         hbuf[r, 0, 1:nx, ny + 7, :] = h0 - COURANT * ye[r, 1, 0:last_x]
@@ -271,39 +328,7 @@
         hbuf[r, 0, 1 : nx + 1, 7, :] = yp[r, 0] - COURANT * ye_out[r, 1] + edge
         hbuf[r, 2, 1 : nx + 1, 7, :] = yp[r, 1] + COURANT * ye_out[r, 0]
 
-    def e_plane(x, carry):
-        m = matb[x]
-        coefficient = jnp.where(
-            m == 0, COURANT / PERMITTIVITIES[0],
-            jnp.where(m == 1, COURANT / PERMITTIVITIES[1],
-                      jnp.where(m == 2, COURANT / PERMITTIVITIES[2], COURANT / PERMITTIVITIES[3])),
-        ).astype(F32)
-        cells = []
-        for r in range(2):
-            h0 = hbuf[r, 0, x + 1, 8 : ny + 8, :]
-            h1 = hbuf[r, 1, x + 1, 8 : ny + 8, :]
-            h2 = hbuf[r, 2, x + 1, 8 : ny + 8, :]
-
-            def down_z(value, c):
-                return jnp.where(lane == 0, below[r, c, x], pltpu.roll(value, 1, 1))
-
-            curl_x = (h2 - hbuf[r, 2, x + 1, 7 : ny + 7, :]) - (h1 - down_z(h1, 1))
-            curl_y = (h0 - down_z(h0, 0)) - (h2 - hbuf[r, 2, x, 8 : ny + 8, :])
-            curl_z = (h1 - hbuf[r, 1, x, 8 : ny + 8, :]) - (h0 - hbuf[r, 0, x + 1, 7 : ny + 7, :])
-            fields = []
-            for c, curl in enumerate((curl_x, curl_y, curl_z)):
-                new_e = ebuf[r, c, x, 0:ny, :] + coefficient * curl
-                ebuf[r, c, x, 0:ny, :] = new_e
-                fields.append(new_e)
-            cells.append(fields)
-        total = gbuf[x]
-        for c in range(3):
-            fwd, adj = cells[0][c], cells[1][c]
-            total = total + (fwd * (ubuf[c, x] + squares * adj) + adj * vbuf[c, x])
-        prod[pl.ds(pl.multiple_of(x * ny, ny) if not isinstance(x, int) else x * ny, ny), :] = total
-        return carry
-
-    lax.fori_loop(1, last_x, e_plane, 0, unroll=2)
+    lax.fori_loop(1, last_x, outer_rows, 0, unroll=2)
 
     sent_xe.wait()
     sent_xp.wait()
@@ -332,8 +357,8 @@
         corner = jnp.where(row == ny - 1, COURANT * xya[r : r + 1, :], 0.0)
         hbuf[r, 2, 0, 8 : ny + 8, :] = xp[r, 1] - COURANT * ebuf[r, 1, 0, 0:ny, :] + corner
 
-    e_plane(0, 0)
-    e_plane(last_x, 0)
+    e_rows(0, 0, ny)
+    e_rows(last_x, 0, ny)
 
     sums = lax.dot_general(
         onehot, prod[...], (((1,), (1,)), ((), ())),

time: 19.8 us -> 19.6 us (0.990); the launches traced: 19.5 us -> 19.5 us
  no operation moved by 1% of the time
where the time goes in v6:
time: 19.6 us; the launch traced here: 19.5 us
  Pallas kernels  18.9 us (96%)
  between operations  0.64 us (3%)
    pallas_call x1, Pallas kernels, shards(): pl.pallas_call(step_kernel, name='yee_step', out_shape=(pltpu.VMEM(padded...  17.1 us
    pallas_call x1, Pallas kernels, shards(): pl.pallas_call(store_kernel, name='store_fields', out_shape=(field, field...  1.71 us

profile of v6, /device:TPU:16, one launch (start us, length us, event | category | flops | bytes accessed | tf_op | source)
XLA Modules:
  0.0 19.5 jit_solution(12762783269895562029)
XLA Ops:
  0.6 17.1 %yee_step.1 = (f32[2,3,17,40,128]{4,3,2,1,0:T(8,128)S(1)}, f32[2,3,17,40,128]{4,3,2,1,0:T(8,128)S(1)}, f32[8,16,32]{2,1,0:T(8,128)S(1)}) custom-call(f32[3,16,32,128]{3,2,1,0:T(8,128)} %ef.1, f32[3,16,32,128]{3,2,1,0:T(8,128)} %hf.1, f32[3,16,32,128]{3,2,1,0:T(8,128)} %ea.1, f32[3,16,32,128]{3,2,1,0:T(8,128)} %ha.1, s32[16,32,128]{2,1,0:T(8,128)} %mat.1, ...), custom_call_target="tpu_custom_call" | custom-call | tf_op jit(solution)/shard_map/yee_step/pallas_call | solution.py:401
  17.8 1.7 %store_fields.1 = (f32[3,16,32,128]{3,2,1,0:T(8,128)}, f32[3,16,32,128]{3,2,1,0:T(8,128)}, f32[3,16,32,128]{3,2,1,0:T(8,128)}, f32[3,16,32,128]{3,2,1,0:T(8,128)}, f32[8,16,32]{2,1,0:T(8,128)}) custom-call(f32[2,3,17,40,128]{4,3,2,1,0:T(8,128)S(1)} %get-tuple-element.8.ebuf, f32[2,3,17,40,128]{4,3,2,1,0:T(8,128)S(1)} %get-tuple-element.9.hbuf, ...), custom_call_target="tpu_custom_call" | custom-call | tf_op jit(solution)/shard_map/store_fields/pallas_call | solution.py:452

commit v7 on v6

--- a/solution.py
+++ b/solution.py
@@ -304,7 +304,7 @@
         e_rows(x, ny - ny // 4, ny // 4)
         return carry
 
-    lax.fori_loop(1, last_x, middle_rows, 0, unroll=2)
+    lax.fori_loop(1, last_x, middle_rows, 0, unroll=7)
 
     sent_yz.wait()
     sent_ye.wait()
@@ -328,7 +328,7 @@
         hbuf[r, 0, 1 : nx + 1, 7, :] = yp[r, 0] - COURANT * ye_out[r, 1] + edge
         hbuf[r, 2, 1 : nx + 1, 7, :] = yp[r, 1] + COURANT * ye_out[r, 0]
 
-    lax.fori_loop(1, last_x, outer_rows, 0, unroll=2)
+    lax.fori_loop(1, last_x, outer_rows, 0, unroll=7)
 
     sent_xe.wait()
     sent_xp.wait()

time: 19.6 us -> 19.6 us (level)
  no operation moved by 1% of the time
where the time goes in v7:
time: 19.6 us; the launch traced here: 19.5 us
  Pallas kernels  18.9 us (96%)
  between operations  0.64 us (3%)
    pallas_call x1, Pallas kernels, shards(): pl.pallas_call(step_kernel, name='yee_step', out_shape=(pltpu.VMEM(padded...  17.1 us
    pallas_call x1, Pallas kernels, shards(): pl.pallas_call(store_kernel, name='store_fields', out_shape=(field, field...  1.71 us

profile of v7, /device:TPU:16, one launch (start us, length us, event | category | flops | bytes accessed | tf_op | source)
XLA Modules:
  0.0 19.5 jit_solution(16294293861463197097)
XLA Ops:
  0.6 17.1 %yee_step.1 = (f32[2,3,17,40,128]{4,3,2,1,0:T(8,128)S(1)}, f32[2,3,17,40,128]{4,3,2,1,0:T(8,128)S(1)}, f32[8,16,32]{2,1,0:T(8,128)S(1)}) custom-call(f32[3,16,32,128]{3,2,1,0:T(8,128)} %ef.1, f32[3,16,32,128]{3,2,1,0:T(8,128)} %hf.1, f32[3,16,32,128]{3,2,1,0:T(8,128)} %ea.1, f32[3,16,32,128]{3,2,1,0:T(8,128)} %ha.1, s32[16,32,128]{2,1,0:T(8,128)} %mat.1, ...), custom_call_target="tpu_custom_call" | custom-call | tf_op jit(solution)/shard_map/yee_step/pallas_call | solution.py:401
  17.8 1.7 %store_fields.1 = (f32[3,16,32,128]{3,2,1,0:T(8,128)}, f32[3,16,32,128]{3,2,1,0:T(8,128)}, f32[3,16,32,128]{3,2,1,0:T(8,128)}, f32[3,16,32,128]{3,2,1,0:T(8,128)}, f32[8,16,32]{2,1,0:T(8,128)}) custom-call(f32[2,3,17,40,128]{4,3,2,1,0:T(8,128)S(1)} %get-tuple-element.8.ebuf, f32[2,3,17,40,128]{4,3,2,1,0:T(8,128)S(1)} %get-tuple-element.9.hbuf, ...), custom_call_target="tpu_custom_call" | custom-call | tf_op jit(solution)/shard_map/store_fields/pallas_call | solution.py:452
